TPU v7x, 32 devices: a whole 2x2x4 slice. The times are simulated.
32 devices in a mesh: groups: 2 (over y), blk: 8 (over z, x), rep: 2 (over core).
Axes of the slice: x: 2, y: 2, z: 4, core: 2. Of those that a mesh axis runs over, the one named last changes fastest.
Arguments:
- tokens: bfloat16 [16384, 1024], P(('groups', 'blk', 'rep')), parts along dimension 0, may hold values from -6 to 6
- hidden_grad: bfloat16 [16384, 4096], P(('groups', 'blk', 'rep')), parts along dimension 0, may hold values from -6 to 6
- weights: bfloat16 [2, 4096, 1024], P(None, 'blk', 'rep'), may hold values from -0.1875 to 0.1875
- first_moment: float32 [2, 8192, 1024], P(None, ('groups', 'blk'), 'rep'), parts along dimension 1, may hold values from -0.0014648438 to 0.0014648438
- second_moment: float32 [2, 8192, 1024], P(None, ('groups', 'blk'), 'rep'), parts along dimension 1, may hold values from 1e-09 to 1e-07
Outputs:
- hidden: bfloat16 [16384, 4096], P(('groups', 'blk', 'rep')), parts along dimension 0
- adam_step: float32 [2, 8192, 1024], P(None, ('groups', 'blk')), parts along dimension 1
There are 2 independent parts, one for each index of `groups`. A program takes and returns all parts, laid end to end along the dimension named above; an argument that names none is the same for every part. Nothing has to cross between parts.
All inputs are finite; a program needn't handle non-finite values.
Results may differ from a plain program's by a relative error of at most 0.0034.
Values may be sent and summed in bfloat16 or wider, within the bound.
A program may use at most 128 MiB of HBM per device.

v0:
```python
import functools

import jax
import jax.numpy as jnp
from jax import lax
from jax.experimental import pallas as pl
from jax.experimental.pallas import tpu as pltpu
from jax.sharding import PartitionSpec as P

clip_norm = 1.0
beta_one = 0.9
beta_two = 0.95
step_count = 10.0
adam_eps = 1e-08
decay_rate = 0.1


def shifted(value, axis, by):
    devices = lax.axis_size(axis)
    return lax.ppermute(value, axis, [(i, (i + by) % devices) for i in range(devices)])


def swiglu_terms(tokens, incoming_grad, gate_rows, up_rows):
    contract = (((1,), (1,)), ((), ()))
    gate = lax.dot_general(tokens, gate_rows, contract, preferred_element_type=jnp.float32)
    upper = lax.dot_general(tokens, up_rows, contract, preferred_element_type=jnp.float32)
    sigma = jax.nn.sigmoid(gate)
    activated = gate * sigma
    hidden = (activated * upper).astype(jnp.bfloat16)
    incoming = incoming_grad.astype(jnp.float32)
    gate_grad = (incoming * upper * sigma * (1.0 + gate * (1.0 - sigma))).astype(jnp.bfloat16)
    up_grad = (incoming * activated).astype(jnp.bfloat16)
    return (hidden, gate_grad, up_grad)


def adam_update(gradient, first_moment, second_moment, weights, norm_sq):
    clip_scale = jnp.minimum(1.0, clip_norm / jnp.sqrt(norm_sq))
    clipped = gradient * clip_scale
    first = beta_one * first_moment + (1.0 - beta_one) * clipped
    second = beta_two * second_moment + (1.0 - beta_two) * clipped * clipped
    first_hat = first / (1.0 - beta_one**step_count)
    second_hat = second / (1.0 - beta_two**step_count)
    return first_hat / (jnp.sqrt(second_hat) + adam_eps) + decay_rate * weights.astype(jnp.float32)


def on_device(tokens, hidden_grad, weights, first_moment, second_moment):
    unit_count = weights.shape[1]
    token_count = tokens.shape[0]
    slot_count = hidden_grad.shape[1] // unit_count
    own_full = lax.all_gather(weights, "rep", axis=2, tiled=True)
    slot_grads = jnp.swapaxes(hidden_grad.reshape(token_count, slot_count, unit_count), 0, 1)
    contract = (((1,), (0,)), ((), ()))

    def grad_term(gate_grad, up_grad):
        paired = jnp.stack([gate_grad, up_grad], axis=0)
        return lax.dot_general(paired, tokens, contract, preferred_element_type=jnp.float32)

    zero_sums = jnp.zeros((2, unit_count, tokens.shape[1]), jnp.float32)

    def visit(panel_rows, slot_grad):
        hidden, gate_grad, up_grad = swiglu_terms(tokens, slot_grad, panel_rows[0], panel_rows[1])
        arrived = shifted(panel_rows, "blk", 1)
        return (arrived, (hidden, gate_grad, up_grad))

    _, (hidden_slots, gate_slots, up_slots) = lax.scan(visit, own_full, slot_grads)

    def collect(running, grads_pair):
        arrived = shifted(running, "blk", -1)
        return (arrived + grad_term(grads_pair[0], grads_pair[1]), None)

    owned_sums, _ = lax.scan(collect, zero_sums, (gate_slots, up_slots), reverse=True)
    hidden = jnp.swapaxes(hidden_slots, 0, 1).reshape(token_count, slot_count * unit_count)
    gradient = lax.psum_scatter(owned_sums, "rep", scatter_dimension=2, tiled=True)
    norm_sq = lax.psum(jnp.sum(gradient * gradient), ("blk", "rep"))
    update = adam_update(gradient, first_moment, second_moment, weights, norm_sq)
    adam_step = lax.all_gather(update, "rep", axis=2, tiled=True)
    return (hidden, adam_step)


def total_kernel(devices, part_ref, out_ref, slots, send_sem, recv_sem):
    me = lax.axis_index("blk") * 2 + lax.axis_index("rep")

    def place(by):
        peer = (me + by) % devices
        return {"blk": peer // 2, "rep": peer % 2}

    barrier = pltpu.get_barrier_semaphore()
    for by in range(1, devices):
        pl.semaphore_signal(barrier, inc=1, device_id=place(by), device_id_type=pl.DeviceIdType.MESH)
    pl.semaphore_wait(barrier, devices - 1)
    slots[me] = part_ref[...]
    copies = []
    for by in range(1, devices):
        copy = pltpu.make_async_remote_copy(
            src_ref=part_ref,
            dst_ref=slots.at[me],
            send_sem=send_sem.at[by],
            recv_sem=recv_sem.at[by],
            device_id=place(by),
            device_id_type=pl.DeviceIdType.MESH,
        )
        copy.start()
        copies.append(copy)
    for copy in copies:
        copy.wait()
    total = slots[0]
    for i in range(1, devices):
        total = total + slots[i]
    out_ref[...] = total


def summed(value):
    devices = lax.axis_size("blk") * lax.axis_size("rep")
    return pl.pallas_call(
        functools.partial(total_kernel, devices),
        out_shape=jax.ShapeDtypeStruct((8, 128), jnp.float32),
        in_specs=[pl.BlockSpec(memory_space=pltpu.VMEM)],
        out_specs=pl.BlockSpec(memory_space=pltpu.VMEM),
        scratch_shapes=[
            pltpu.VMEM((devices, 8, 128), jnp.float32),
            pltpu.SemaphoreType.DMA((devices,)),
            pltpu.SemaphoreType.DMA((devices,)),
        ],
        compiler_params=pltpu.CompilerParams(collective_id=0, has_side_effects=True),
    )(jnp.broadcast_to(value, (8, 128)))


def adam_kernel(norm_ref, *refs):
    own, other, out_ref = refs[:4], refs[4:8], refs[8]
    features = own[0].shape[-1]
    norm_sq = norm_ref[0:1, 0:1]

    def write(values, first):
        gradient, first_moment, second_moment, weights = (ref[0] for ref in values)
        out_ref[0, :, first : first + features] = adam_update(
            gradient, first_moment, second_moment, weights, norm_sq
        )

    rep = lax.axis_index("rep")

    @pl.when(rep == 0)
    def _():
        write(own, 0)
        write(other, features)

    @pl.when(rep != 0)
    def _():
        write(other, 0)
        write(own, features)


def adam_all(norm_sq, own, other):
    pair, units, features = own[0].shape
    tile = min(units, 128)
    block = pl.BlockSpec((1, tile, features), lambda i, j: (i, j, 0))
    return pl.pallas_call(
        adam_kernel,
        grid=(pair, units // tile),
        out_shape=jax.ShapeDtypeStruct((pair, units, 2 * features), jnp.float32),
        in_specs=[pl.BlockSpec((8, 128), lambda i, j: (0, 0))] + [block] * 8,
        out_specs=pl.BlockSpec((1, tile, 2 * features), lambda i, j: (i, j, 0)),
        compiler_params=pltpu.CompilerParams(vmem_limit_bytes=24 * 1024 * 1024),
    )(norm_sq, *own, *other)


def ring_order(devices):
    return list(range(0, devices, 2)) + list(range(devices - 1, 0, -2))


def on_ring(tokens, hidden_grad, weights, first_moment, second_moment):
    devices = lax.axis_size("blk")
    half = devices // 2
    units, features = weights.shape[1], weights.shape[2]
    order = ring_order(devices)
    blk, rep = lax.axis_index("blk"), lax.axis_index("rep")
    positions = [order.index(i) for i in range(devices)]
    pos = jnp.array(positions, jnp.int32)[blk]

    def hop(value, by):
        return lax.ppermute(value, "blk", [(order[i], order[(i + by) % devices]) for i in range(devices)])

    def partner(value):
        return lax.ppermute(value, "rep", [(0, 1), (1, 0)])

    own_tokens = lax.dynamic_slice_in_dim(tokens, rep * features, features, 1)
    other_tokens = lax.dynamic_slice_in_dim(tokens, (1 - rep) * features, features, 1)

    panels = {0: weights}
    for k in range(1, half):
        panels[k] = hop(panels[k - 1], 1)
        panels[-k] = hop(panels[1 - k], -1)
    panels[half] = (hop(panels[half - 1][0], 1), hop(panels[1 - half][1], -1))

    def rows(own, other):
        contract = (((1,), (1,)), ((), ()))
        return lax.dot_general(own_tokens, own, contract, preferred_element_type=jnp.float32) + lax.dot_general(
            other_tokens, other, contract, preferred_element_type=jnp.float32
        )

    def slot_of(distance):
        owner = jnp.array(order, jnp.int32)[(pos - distance) % devices]
        return (blk - owner) % devices

    sequence = [0]
    for k in range(1, half):
        sequence += [k, -k]
    sequence.append(half)
    hidden = jnp.zeros(hidden_grad.shape, hidden_grad.dtype)
    grads = {}
    for d in sequence:
        if d == half:
            gate_other, up_other = partner(panels[d][0]), partner(panels[d][1])
        else:
            gate_other, up_other = partner(panels[d])
        gate, upper = rows(panels[d][0], gate_other), rows(panels[d][1], up_other)
        start = slot_of(d) * units
        incoming = lax.dynamic_slice_in_dim(hidden_grad, start, units, 1).astype(jnp.float32)
        sigma = jax.nn.sigmoid(gate)
        activated = gate * sigma
        hidden = lax.dynamic_update_slice_in_dim(hidden, (activated * upper).astype(jnp.bfloat16), start, 1)
        gate_grad = (incoming * upper * sigma * (1.0 + gate * (1.0 - sigma))).astype(jnp.bfloat16)
        up_grad = (incoming * activated).astype(jnp.bfloat16)
        grads[d] = (gate_grad, up_grad)

    def term(d, which):
        contract = (((0,), (0,)), ((), ()))
        away = lax.dot_general(grads[d][which], other_tokens, contract, preferred_element_type=jnp.float32)
        kept = lax.dot_general(grads[d][which], own_tokens, contract, preferred_element_type=jnp.float32)
        return kept + partner(away.astype(jnp.bfloat16)).astype(jnp.float32)

    def chain(sign):
        running = [None, None]
        lead = 0 if sign > 0 else 1
        running[lead] = term(half, lead)
        arrived = [None, None]
        arrived[lead] = hop(running[lead].astype(jnp.bfloat16), -sign)
        for k in range(half - 1, 0, -1):
            for which in range(2):
                running[which] = term(sign * k, which)
                if arrived[which] is not None:
                    running[which] = running[which] + arrived[which].astype(jnp.float32)
            arrived = [hop(value.astype(jnp.bfloat16), -sign) for value in running]
        return arrived

    up_way, down_way = chain(1), chain(-1)
    gradient = jnp.stack(
        [term(0, w) + up_way[w].astype(jnp.float32) + down_way[w].astype(jnp.float32) for w in range(2)]
    )
    norm_sq = summed(jnp.sum(gradient * gradient))
    own = (gradient, first_moment, second_moment, weights)
    update = adam_all(norm_sq, own, tuple(partner(value) for value in own))
    return (hidden, update)


def solution(mesh):
    placed = (
        P(("groups", "blk", "rep"), None),
        P(("groups", "blk", "rep"), None),
        P(None, "blk", "rep"),
        P(None, ("groups", "blk"), "rep"),
        P(None, ("groups", "blk"), "rep"),
    )
    devices = mesh.shape["blk"]

    def program(tokens, hidden_grad, weights, first_moment, second_moment):
        slots = hidden_grad.shape[1] * devices // weights.shape[1]
        whole_cycle = slots == devices and devices % 2 == 0 and devices >= 4 and mesh.shape["rep"] == 2
        step = jax.shard_map(
            on_ring if whole_cycle else on_device,
            mesh=mesh,
            in_specs=placed,
            out_specs=(P(("groups", "blk", "rep"), None), P(None, ("groups", "blk"), None)),
            check_vma=False,
        )
        return step(tokens, hidden_grad, weights, first_moment, second_moment)

    return program
```

profile of v0, /device:TPU:0, one launch (start us, length us, event | category | flops | bytes accessed | tf_op | source)
XLA Modules:
  0.0 241.7 jit_solution(5381904930183775317)
XLA Ops:
  0.6 3.1 %collective-permute-start.1 = (bf16[2,512,512]{2,1,0:T(8,128)(2,1)}, bf16[2,512,512]{2,1,0:T(8,128)(2,1)}, u32[]{:S(2)}, u32[]{:S(2)}) collective-permute-start(bf16[2,512,512]{2,1,0:T(8,128)(2,1)} %refs_3_.1), channel_id=1, source_target_pairs={{0,4},{4,8},{8,12},{12,14},{14,10},{10,6},{6,2},{2,0},{1,5},{5,9},... | collective-permute-start | bytes 3145736 | tf_op jit(solution)/shard_map/ppermute | solution.py:180
  3.7 1.2 dynamic_slice.59
  11.6 1.6 fusion.84
  18.3 1.5 fusion.60
  19.9 1.5 fusion.58
  21.4 5.7 %collective-permute-done.1 = bf16[2,512,512]{2,1,0:T(8,128)(2,1)} collective-permute-done((bf16[2,512,512]{2,1,0:T(8,128)(2,1)}, bf16[2,512,512]{2,1,0:T(8,128)(2,1)}, u32[]{:S(2)}, u32[]{:S(2)}) %collective-permute-start.1) | collective-permute-done | bytes 1048608 | tf_op jit(solution)/shard_map/ppermute | solution.py:180
  27.1 1.8 collective-permute-start.5
  29.4 1.5 fusion.57
  31.4 1.5 fusion.56
  33.9 2.5 %broadcast_in_dim.6 = bf16[512,4096]{1,0:T(8,128)(2,1)} broadcast(bf16[]{:T(256)} %constant.101.clone.1), dimensions={} | broadcast | bytes 4194306 | tf_op jit(solution)/shard_map/broadcast_in_dim | solution.py:208
  36.4 1.4 fusion.40
  37.8 15.1 %collective-permute-done.5 = bf16[2,512,512]{2,1,0:T(8,128)(2,1)S(1)} collective-permute-done((bf16[2,512,512]{2,1,0:T(8,128)(2,1)}, bf16[2,512,512]{2,1,0:T(8,128)(2,1)S(1)}, u32[]{:S(2)}, u32[]{:S(2)}) %collective-permute-start.5) | collective-permute-done | bytes 1048608 | tf_op jit(solution)/shard_map/ppermute | solution.py:180
  52.9 1.8 collective-permute-start.9
  56.7 1.4 fusion.41
  59.0 1.4 fusion.42
  60.9 17.6 %collective-permute-done.9 = bf16[2,512,512]{2,1,0:T(8,128)(2,1)S(1)} collective-permute-done((bf16[2,512,512]{2,1,0:T(8,128)(2,1)S(1)}, bf16[2,512,512]{2,1,0:T(8,128)(2,1)S(1)}, u32[]{:S(2)}, u32[]{:S(2)}) %collective-permute-start.9) | collective-permute-done | bytes 1048608 | tf_op jit(solution)/shard_map/ppermute | solution.py:180
  78.5 1.9 collective-permute-start.13
  83.9 1.4 fusion.43
  85.3 1.4 fusion.44
  87.7 4.4 %collective-permute-done.13 = bf16[512,512]{1,0:T(8,128)(2,1)S(1)} collective-permute-done((bf16[512,512]{1,0:T(8,128)(2,1)S(1)}, bf16[512,512]{1,0:T(8,128)(2,1)S(1)}, u32[]{:S(2)}, u32[]{:S(2)}) %collective-permute-start.13) | collective-permute-done | bytes 524320 | tf_op jit(solution)/shard_map/ppermute | solution.py:180
  92.1 2.3 collective-permute-done.15
  96.8 1.4 fusion.45
  98.3 1.4 fusion.46
  100.6 1.3 fusion.26
  103.8 1.4 fusion.47
  105.2 3.8 %fusion.2 = (bf16[512,512]{1,0:T(8,128)(2,1)S(1)}, bf16[512,512]{1,0:T(8,128)(2,1)S(1)}, bf16[512,512]{1,0:T(8,128)(2,1)S(1)}, bf16[512,512]{1,0:T(8,128)(2,1)S(...) fusion(f32[512,512]{1,0:T(8,128)S(1)} %get-tuple-element.41, ...), kind=kLoop, calls=%fused_computation.52 | loop fusion | flops 22020096 | bytes 22020120 | tf_op jit(solution)/shard_map/convert_element_type | solution.py:221
  123.4 1.5 collective-permute-start.43
  126.6 10.8 %collective-permute-done.43 = bf16[512,512]{1,0:T(8,128)(2,1)S(1)} collective-permute-done((bf16[512,512]{1,0:T(8,128)(2,1)S(1)}, bf16[512,512]{1,0:T(8,128)(2,1)S(1)}, u32[]{:S(2)}, u32[]{:S(2)}) %collective-permute-start.43) | collective-permute-done | bytes 524320 | tf_op jit(solution)/shard_map/ppermute | solution.py:180
  137.4 1.5 collective-permute-start.29
  140.3 10.2 %collective-permute-done.29 = bf16[512,512]{1,0:T(8,128)(2,1)S(1)} collective-permute-done((bf16[512,512]{1,0:T(8,128)(2,1)S(1)}, bf16[512,512]{1,0:T(8,128)(2,1)S(1)}, u32[]{:S(2)}, u32[]{:S(2)}) %collective-permute-start.29) | collective-permute-done | bytes 524320 | tf_op jit(solution)/shard_map/ppermute | solution.py:180
  150.5 1.5 collective-permute-start.44
  154.4 8.3 %collective-permute-done.44 = bf16[512,512]{1,0:T(8,128)(2,1)S(1)} collective-permute-done((bf16[512,512]{1,0:T(8,128)(2,1)S(1)}, bf16[512,512]{1,0:T(8,128)(2,1)S(1)}, u32[]{:S(2)}, u32[]{:S(2)}) %collective-permute-start.44) | collective-permute-done | bytes 524320 | tf_op jit(solution)/shard_map/ppermute | solution.py:180
  163.3 5.1 %collective-permute-done.37 = bf16[512,512]{1,0:T(8,128)(2,1)S(1)} collective-permute-done((bf16[512,512]{1,0:T(8,128)(2,1)S(1)}, bf16[512,512]{1,0:T(8,128)(2,1)S(1)}, u32[]{:S(2)}, u32[]{:S(2)}) %collective-permute-start.37) | collective-permute-done | bytes 524320 | tf_op jit(solution)/shard_map/ppermute | solution.py:180
  168.4 1.5 collective-permute-start.30
  170.3 8.0 %collective-permute-done.23 = bf16[512,512]{1,0:T(8,128)(2,1)S(1)} collective-permute-done((bf16[512,512]{1,0:T(8,128)(2,1)S(1)}, bf16[512,512]{1,0:T(8,128)(2,1)S(1)}, u32[]{:S(2)}, u32[]{:S(2)}) %collective-permute-start.23) | collective-permute-done | bytes 524320 | tf_op jit(solution)/shard_map/ppermute | solution.py:180
  178.3 1.5 collective-permute-start.45
  181.3 9.6 %collective-permute-done.45 = bf16[512,512]{1,0:T(8,128)(2,1)S(1)} collective-permute-done((bf16[512,512]{1,0:T(8,128)(2,1)S(1)}, bf16[512,512]{1,0:T(8,128)(2,1)S(1)}, u32[]{:S(2)}, u32[]{:S(2)}) %collective-permute-start.45) | collective-permute-done | bytes 524320 | tf_op jit(solution)/shard_map/ppermute | solution.py:180
  191.6 1.6 collective-permute-start.31
  193.2 1.8 collective-permute-done.24
  195.0 1.5 collective-permute-start.46
  197.8 8.4 %collective-permute-done.38 = bf16[512,512]{1,0:T(8,128)(2,1)S(1)} collective-permute-done((bf16[512,512]{1,0:T(8,128)(2,1)S(1)}, bf16[512,512]{1,0:T(8,128)(2,1)S(1)}, u32[]{:S(2)}, u32[]{:S(2)}) %collective-permute-start.38) | collective-permute-done | bytes 524320 | tf_op jit(solution)/shard_map/ppermute | solution.py:180
  206.2 8.1 %collective-permute-done.46 = bf16[512,512]{1,0:T(8,128)(2,1)S(1)} collective-permute-done((bf16[512,512]{1,0:T(8,128)(2,1)S(1)}, bf16[512,512]{1,0:T(8,128)(2,1)S(1)}, u32[]{:S(2)}, u32[]{:S(2)}) %collective-permute-start.46) | collective-permute-done | bytes 524320 | tf_op jit(solution)/shard_map/ppermute | solution.py:180
  214.6 2.4 collective-permute-done.25
  218.5 1.3 broadcast_in_dim.7.part_ref
  219.8 8.0 %shard_map.149.norm_ref = f32[8,128]{1,0:T(8,128)} custom-call(f32[8,128]{1,0:T(8,128)} %broadcast_in_dim.7.part_ref), custom_call_target="tpu_custom_call" | custom-call | tf_op jit(solution)/shard_map/pallas_call | solution.py:114
  227.9 1.2 copy-done.1
  229.1 1.2 copy-done.3
  231.0 10.7 %shard_map.150 = f32[2,512,1024]{2,1,0:T(8,128)} custom-call(f32[8,128]{1,0:T(8,128)S(1)} %copy-done.4, f32[2,512,512]{2,1,0:T(8,128)S(1)} %get-tuple-element.30.refs_0_, f32[2,512,512]{2,1,0:T(8,128)} %refs_1_.1, f32[2,512,512]{2,1,0:T(8,128)} %refs_2_.1, bf16[2,512,512]{2,1,0:T(8,128)(2,1)S(1)} %copy-done.1, ...), custom_call_target="tpu_custom_call" | custom-call | tf_op jit(solution)/shard_map/pallas_call | solution.py:156
  (151 shorter events, 41.3 us)
Async XLA Ops:
  0.6 26.5 %collective-permute-start.1 = (bf16[2,512,512]{2,1,0:T(8,128)(2,1)}, bf16[2,512,512]{2,1,0:T(8,128)(2,1)}, u32[]{:S(2)}, u32[]{:S(2)}) collective-permute-start(bf16[2,512,512]{2,1,0:T(8,128)(2,1)} %refs_3_.1), channel_id=1, source_target_pairs={{0,4},{4,8},{8,12},{12,14},{14,10},{10,6},{6,2},{2,0},{1,5},{5,9},... | collective-permute-start | bytes 3145736 | tf_op jit(solution)/shard_map/ppermute | solution.py:180
  3.7 25.2 %collective-permute-start.3 = (bf16[2,512,512]{2,1,0:T(8,128)(2,1)}, bf16[2,512,512]{2,1,0:T(8,128)(2,1)S(1)}, u32[]{:S(2)}, u32[]{:S(2)}) collective-permute-start(bf16[2,512,512]{2,1,0:T(8,128)(2,1)} %refs_3_.1), channel_id=1, source_target_pairs={{0,2},{4,0},{8,4},{12,8},{14,12},{10,14},{6,10},{2,6},{1,3},{5,1},... | collective-permute-start | bytes 3145736 | tf_op jit(solution)/shard_map/ppermute | solution.py:180
  3.7 27.2 %collective-permute-start = (bf16[2,512,512]{2,1,0:T(8,128)(2,1)}, bf16[2,512,512]{2,1,0:T(8,128)(2,1)S(1)}, u32[]{:S(2)}, u32[]{:S(2)}) collective-permute-start(bf16[2,512,512]{2,1,0:T(8,128)(2,1)} %refs_3_.1), channel_id=1, source_target_pairs={{0,1},{1,0},{2,3},{3,2},{4,5},{5,4},{6,7},{7,6},{8,9},{9,8},{10,11... | collective-permute-start | bytes 3145736 | tf_op jit(solution)/shard_map/ppermute | solution.py:183
  27.1 28.3 %collective-permute-start.2 = (bf16[2,512,512]{2,1,0:T(8,128)(2,1)}, bf16[2,512,512]{2,1,0:T(8,128)(2,1)S(1)}, u32[]{:S(2)}, u32[]{:S(2)}) collective-permute-start(bf16[2,512,512]{2,1,0:T(8,128)(2,1)} %collective-permute-done.1), channel_id=1, source_target_pairs={{0,1},{1,0},{2,3},{3,2},{4,5},{5,4},{6,7},{7,6},{8,9},{9,8},{10,11... | collective-permute-start | bytes 3145736 | tf_op jit(solution)/shard_map/ppermute | solution.py:183
  27.1 25.8 %collective-permute-start.5 = (bf16[2,512,512]{2,1,0:T(8,128)(2,1)}, bf16[2,512,512]{2,1,0:T(8,128)(2,1)S(1)}, u32[]{:S(2)}, u32[]{:S(2)}) collective-permute-start(bf16[2,512,512]{2,1,0:T(8,128)(2,1)} %collective-permute-done.1), channel_id=1, source_target_pairs={{0,4},{4,8},{8,12},{12,14},{14,10},{10,6},{6,2},{2,0},{1,5},{5,9},... | collective-permute-start | bytes 3145736 | tf_op jit(solution)/shard_map/ppermute | solution.py:180
  28.9 27.2 %collective-permute-start.4 = (bf16[2,512,512]{2,1,0:T(8,128)(2,1)S(1)}, bf16[2,512,512]{2,1,0:T(8,128)(2,1)S(1)}, u32[]{:S(2)}, u32[]{:S(2)}) collective-permute-start(bf16[2,512,512]{2,1,0:T(8,128)(2,1)S(1)} %collective-permute-done.3), channel_id=1, source_target_pairs={{0,1},{1,0},{2,3},{3,2},{4,5},{5,4},{6,7},{7,6},{8,9},{9,8},{10,11... | collective-permute-start | bytes 3145736 | tf_op jit(solution)/shard_map/ppermute | solution.py:183
  29.2 25.6 %collective-permute-start.7 = (bf16[2,512,512]{2,1,0:T(8,128)(2,1)S(1)}, bf16[2,512,512]{2,1,0:T(8,128)(2,1)S(1)}, u32[]{:S(2)}, u32[]{:S(2)}) collective-permute-start(bf16[2,512,512]{2,1,0:T(8,128)(2,1)S(1)} %collective-permute-done.3), channel_id=1, source_target_pairs={{0,2},{4,0},{8,4},{12,8},{14,12},{10,14},{6,10},{2,6},{1,3},{5,1},... | collective-permute-start | bytes 3145736 | tf_op jit(solution)/shard_map/ppermute | solution.py:180
  52.9 29.5 %collective-permute-start.6 = (bf16[2,512,512]{2,1,0:T(8,128)(2,1)S(1)}, bf16[2,512,512]{2,1,0:T(8,128)(2,1)S(1)}, u32[]{:S(2)}, u32[]{:S(2)}) collective-permute-start(bf16[2,512,512]{2,1,0:T(8,128)(2,1)S(1)} %collective-permute-done.5), channel_id=1, source_target_pairs={{0,1},{1,0},{2,3},{3,2},{4,5},{5,4},{6,7},{7,6},{8,9},{9,8},{10,11... | collective-permute-start | bytes 3145736 | tf_op jit(solution)/shard_map/ppermute | solution.py:183
  52.9 25.6 %collective-permute-start.9 = (bf16[2,512,512]{2,1,0:T(8,128)(2,1)S(1)}, bf16[2,512,512]{2,1,0:T(8,128)(2,1)S(1)}, u32[]{:S(2)}, u32[]{:S(2)}) collective-permute-start(bf16[2,512,512]{2,1,0:T(8,128)(2,1)S(1)} %collective-permute-done.5), channel_id=1, source_target_pairs={{0,4},{4,8},{8,12},{12,14},{14,10},{10,6},{6,2},{2,0},{1,5},{5,9},... | collective-permute-start | bytes 3145736 | tf_op jit(solution)/shard_map/ppermute | solution.py:180
  54.7 28.7 %collective-permute-start.8 = (bf16[2,512,512]{2,1,0:T(8,128)(2,1)S(1)}, bf16[2,512,512]{2,1,0:T(8,128)(2,1)S(1)}, u32[]{:S(2)}, u32[]{:S(2)}) collective-permute-start(bf16[2,512,512]{2,1,0:T(8,128)(2,1)S(1)} %collective-permute-done.7), channel_id=1, source_target_pairs={{0,1},{1,0},{2,3},{3,2},{4,5},{5,4},{6,7},{7,6},{8,9},{9,8},{10,11... | collective-permute-start | bytes 3145736 | tf_op jit(solution)/shard_map/ppermute | solution.py:183
  55.4 25.4 %collective-permute-start.11 = (bf16[2,512,512]{2,1,0:T(8,128)(2,1)S(1)}, bf16[2,512,512]{2,1,0:T(8,128)(2,1)S(1)}, u32[]{:S(2)}, u32[]{:S(2)}) collective-permute-start(bf16[2,512,512]{2,1,0:T(8,128)(2,1)S(1)} %collective-permute-done.7), channel_id=1, source_target_pairs={{0,2},{4,0},{8,4},{12,8},{14,12},{10,14},{6,10},{2,6},{1,3},{5,1},... | collective-permute-start | bytes 3145736 | tf_op jit(solution)/shard_map/ppermute | solution.py:180
  78.5 13.6 %collective-permute-start.13 = (bf16[512,512]{1,0:T(8,128)(2,1)S(1)}, bf16[512,512]{1,0:T(8,128)(2,1)S(1)}, u32[]{:S(2)}, u32[]{:S(2)}) collective-permute-start(bf16[512,512]{1,0:T(8,128)(2,1)S(1)} %slice_bitcast_fusion.13), channel_id=1, source_target_pairs={{0,4},{4,8},{8,12},{12,14},{14,10},{10,6},{6,2},{2,0},{1,5},{5,9},... | collective-permute-start | bytes 1572872 | tf_op jit(solution)/shard_map/ppermute | solution.py:180
  80.9 13.5 %collective-permute-start.15 = (bf16[512,512]{1,0:T(8,128)(2,1)S(1)}, bf16[512,512]{1,0:T(8,128)(2,1)S(1)}, u32[]{:S(2)}, u32[]{:S(2)}) collective-permute-start(bf16[512,512]{1,0:T(8,128)(2,1)S(1)} %slice_bitcast_fusion.2), channel_id=1, source_target_pairs={{0,2},{4,0},{8,4},{12,8},{14,12},{10,14},{6,10},{2,6},{1,3},{5,1},... | collective-permute-start | bytes 1572872 | tf_op jit(solution)/shard_map/ppermute | solution.py:180
  81.4 14.5 %collective-permute-start.10 = (bf16[2,512,512]{2,1,0:T(8,128)(2,1)S(1)}, bf16[2,512,512]{2,1,0:T(8,128)(2,1)S(1)}, u32[]{:S(2)}, u32[]{:S(2)}) collective-permute-start(bf16[2,512,512]{2,1,0:T(8,128)(2,1)S(1)} %collective-permute-done.9), channel_id=1, source_target_pairs={{0,1},{1,0},{2,3},{3,2},{4,5},{5,4},{6,7},{7,6},{8,9},{9,8},{10,11... | collective-permute-start | bytes 3145736 | tf_op jit(solution)/shard_map/ppermute | solution.py:183
  82.4 14.0 %collective-permute-start.12 = (bf16[2,512,512]{2,1,0:T(8,128)(2,1)S(1)}, bf16[2,512,512]{2,1,0:T(8,128)(2,1)S(1)}, u32[]{:S(2)}, u32[]{:S(2)}) collective-permute-start(bf16[2,512,512]{2,1,0:T(8,128)(2,1)S(1)} %collective-permute-done.11), channel_id=1, source_target_pairs={{0,1},{1,0},{2,3},{3,2},{4,5},{5,4},{6,7},{7,6},{8,9},{9,8},{10,11... | collective-permute-start | bytes 3145736 | tf_op jit(solution)/shard_map/ppermute | solution.py:183
  94.4 9.4 %collective-permute-start.16 = (bf16[512,512]{1,0:T(8,128)(2,1)S(1)}, bf16[512,512]{1,0:T(8,128)(2,1)S(1)}, u32[]{:S(2)}, u32[]{:S(2)}) collective-permute-start(bf16[512,512]{1,0:T(8,128)(2,1)S(1)} %collective-permute-done.15), channel_id=1, source_target_pairs={{0,1},{1,0},{2,3},{3,2},{4,5},{5,4},{6,7},{7,6},{8,9},{9,8},{10,11... | collective-permute-start | bytes 1572872 | tf_op jit(solution)/shard_map/ppermute | solution.py:183
  116.0 5.4 %collective-permute-start.42 = (bf16[512,512]{1,0:T(8,128)(2,1)S(1)}, bf16[512,512]{1,0:T(8,128)(2,1)S(1)}, u32[]{:S(2)}, u32[]{:S(2)}) collective-permute-start(bf16[512,512]{1,0:T(8,128)(2,1)S(1)} %convolution_convert_fusion), channel_id=1, source_target_pairs={{0,1},{1,0},{2,3},{3,2},{4,5},{5,4},{6,7},{7,6},{8,9},{9,8},{10,11... | collective-permute-start | bytes 1572872 | tf_op jit(solution)/shard_map/ppermute | solution.py:183
  116.6 9.9 %collective-permute-start.41 = (bf16[512,512]{1,0:T(8,128)(2,1)S(1)}, bf16[512,512]{1,0:T(8,128)(2,1)S(1)}, u32[]{:S(2)}, u32[]{:S(2)}) collective-permute-start(bf16[512,512]{1,0:T(8,128)(2,1)S(1)} %convolution_convert_fusion.1), channel_id=1, source_target_pairs={{0,1},{1,0},{2,3},{3,2},{4,5},{5,4},{6,7},{7,6},{8,9},{9,8},{10,11... | collective-permute-start | bytes 1572872 | tf_op jit(solution)/shard_map/ppermute | solution.py:183
  116.7 37.7 %collective-permute-start.40 = (bf16[512,512]{1,0:T(8,128)(2,1)S(1)}, bf16[512,512]{1,0:T(8,128)(2,1)S(1)}, u32[]{:S(2)}, u32[]{:S(2)}) collective-permute-start(bf16[512,512]{1,0:T(8,128)(2,1)S(1)} %convolution_convert_fusion.2), channel_id=1, source_target_pairs={{0,1},{1,0},{2,3},{3,2},{4,5},{5,4},{6,7},{7,6},{8,9},{9,8},{10,11... | collective-permute-start | bytes 1572872 | tf_op jit(solution)/shard_map/ppermute | solution.py:183
  117.6 4.5 %collective-permute-start.35 = (bf16[512,512]{1,0:T(8,128)(2,1)S(1)}, bf16[512,512]{1,0:T(8,128)(2,1)S(1)}, u32[]{:S(2)}, u32[]{:S(2)}) collective-permute-start(bf16[512,512]{1,0:T(8,128)(2,1)S(1)} %convolution_convert_fusion.4), channel_id=1, source_target_pairs={{0,1},{1,0},{2,3},{3,2},{4,5},{5,4},{6,7},{7,6},{8,9},{9,8},{10,11... | collective-permute-start | bytes 1572872 | tf_op jit(solution)/shard_map/ppermute | solution.py:183
  117.7 21.4 %collective-permute-start.34 = (bf16[512,512]{1,0:T(8,128)(2,1)S(1)}, bf16[512,512]{1,0:T(8,128)(2,1)S(1)}, u32[]{:S(2)}, u32[]{:S(2)}) collective-permute-start(bf16[512,512]{1,0:T(8,128)(2,1)S(1)} %convolution_convert_fusion.5), channel_id=1, source_target_pairs={{0,1},{1,0},{2,3},{3,2},{4,5},{5,4},{6,7},{7,6},{8,9},{9,8},{10,11... | collective-permute-start | bytes 1572872 | tf_op jit(solution)/shard_map/ppermute | solution.py:183
  122.1 3.3 %collective-permute-start.21 = (bf16[512,512]{1,0:T(8,128)(2,1)S(1)}, bf16[512,512]{1,0:T(8,128)(2,1)S(1)}, u32[]{:S(2)}, u32[]{:S(2)}) collective-permute-start(bf16[512,512]{1,0:T(8,128)(2,1)S(1)} %convolution_convert_fusion.11), channel_id=1, source_target_pairs={{0,1},{1,0},{2,3},{3,2},{4,5},{5,4},{6,7},{7,6},{8,9},{9,8},{10,11... | collective-permute-start | bytes 1572872 | tf_op jit(solution)/shard_map/ppermute | solution.py:183
  123.4 14.0 %collective-permute-start.43 = (bf16[512,512]{1,0:T(8,128)(2,1)S(1)}, bf16[512,512]{1,0:T(8,128)(2,1)S(1)}, u32[]{:S(2)}, u32[]{:S(2)}) collective-permute-start(bf16[512,512]{1,0:T(8,128)(2,1)S(1)} %add_convert_fusion.3), channel_id=1, source_target_pairs={{0,4},{4,8},{8,12},{12,14},{14,10},{10,6},{6,2},{2,0},{1,5},{5,9},... | collective-permute-start | bytes 1572872 | tf_op jit(solution)/shard_map/ppermute | solution.py:180
  125.4 13.8 %collective-permute-start.36 = (bf16[512,512]{1,0:T(8,128)(2,1)S(1)}, bf16[512,512]{1,0:T(8,128)(2,1)S(1)}, u32[]{:S(2)}, u32[]{:S(2)}) collective-permute-start(bf16[512,512]{1,0:T(8,128)(2,1)S(1)} %add_convert_fusion.6), channel_id=1, source_target_pairs={{0,2},{4,0},{8,4},{12,8},{14,12},{10,14},{6,10},{2,6},{1,3},{5,1},... | collective-permute-start | bytes 1572872 | tf_op jit(solution)/shard_map/ppermute | solution.py:180
  126.5 13.6 %collective-permute-start.27 = (bf16[512,512]{1,0:T(8,128)(2,1)S(1)}, bf16[512,512]{1,0:T(8,128)(2,1)S(1)}, u32[]{:S(2)}, u32[]{:S(2)}) collective-permute-start(bf16[512,512]{1,0:T(8,128)(2,1)S(1)} %convolution_convert_fusion.9), channel_id=1, source_target_pairs={{0,1},{1,0},{2,3},{3,2},{4,5},{5,4},{6,7},{7,6},{8,9},{9,8},{10,11... | collective-permute-start | bytes 1572872 | tf_op jit(solution)/shard_map/ppermute | solution.py:183
  137.4 13.1 %collective-permute-start.29 = (bf16[512,512]{1,0:T(8,128)(2,1)S(1)}, bf16[512,512]{1,0:T(8,128)(2,1)S(1)}, u32[]{:S(2)}, u32[]{:S(2)}) collective-permute-start(bf16[512,512]{1,0:T(8,128)(2,1)S(1)} %add_convert_fusion.9), channel_id=1, source_target_pairs={{0,4},{4,8},{8,12},{12,14},{14,10},{10,6},{6,2},{2,0},{1,5},{5,9},... | collective-permute-start | bytes 1572872 | tf_op jit(solution)/shard_map/ppermute | solution.py:180
  139.2 13.2 %collective-permute-start.20 = (bf16[512,512]{1,0:T(8,128)(2,1)S(1)}, bf16[512,512]{1,0:T(8,128)(2,1)S(1)}, u32[]{:S(2)}, u32[]{:S(2)}) collective-permute-start(bf16[512,512]{1,0:T(8,128)(2,1)S(1)} %convolution_convert_fusion.12), channel_id=1, source_target_pairs={{0,1},{1,0},{2,3},{3,2},{4,5},{5,4},{6,7},{7,6},{8,9},{9,8},{10,11... | collective-permute-start | bytes 1572872 | tf_op jit(solution)/shard_map/ppermute | solution.py:183
  139.2 14.3 %collective-permute-start.22 = (bf16[512,512]{1,0:T(8,128)(2,1)S(1)}, bf16[512,512]{1,0:T(8,128)(2,1)S(1)}, u32[]{:S(2)}, u32[]{:S(2)}) collective-permute-start(bf16[512,512]{1,0:T(8,128)(2,1)S(1)} %add_convert_fusion.13), channel_id=1, source_target_pairs={{0,2},{4,0},{8,4},{12,8},{14,12},{10,14},{6,10},{2,6},{1,3},{5,1},... | collective-permute-start | bytes 1572872 | tf_op jit(solution)/shard_map/ppermute | solution.py:180
  140.1 40.9 %collective-permute-start.39 = (bf16[512,512]{1,0:T(8,128)(2,1)S(1)}, bf16[512,512]{1,0:T(8,128)(2,1)S(1)}, u32[]{:S(2)}, u32[]{:S(2)}) collective-permute-start(bf16[512,512]{1,0:T(8,128)(2,1)S(1)} %convolution_convert_fusion.3), channel_id=1, source_target_pairs={{0,1},{1,0},{2,3},{3,2},{4,5},{5,4},{6,7},{7,6},{8,9},{9,8},{10,11... | collective-permute-start | bytes 1572872 | tf_op jit(solution)/shard_map/ppermute | solution.py:183
  150.5 12.2 %collective-permute-start.44 = (bf16[512,512]{1,0:T(8,128)(2,1)S(1)}, bf16[512,512]{1,0:T(8,128)(2,1)S(1)}, u32[]{:S(2)}, u32[]{:S(2)}) collective-permute-start(bf16[512,512]{1,0:T(8,128)(2,1)S(1)} %add_convert_fusion.2), channel_id=1, source_target_pairs={{0,4},{4,8},{8,12},{12,14},{14,10},{10,6},{6,2},{2,0},{1,5},{5,9},... | collective-permute-start | bytes 1572872 | tf_op jit(solution)/shard_map/ppermute | solution.py:180
  152.3 10.9 %collective-permute-start.33 = (bf16[512,512]{1,0:T(8,128)(2,1)S(1)}, bf16[512,512]{1,0:T(8,128)(2,1)S(1)}, u32[]{:S(2)}, u32[]{:S(2)}) collective-permute-start(bf16[512,512]{1,0:T(8,128)(2,1)S(1)} %convolution_convert_fusion.6), channel_id=1, source_target_pairs={{0,1},{1,0},{2,3},{3,2},{4,5},{5,4},{6,7},{7,6},{8,9},{9,8},{10,11... | collective-permute-start | bytes 1572872 | tf_op jit(solution)/shard_map/ppermute | solution.py:183
  153.6 14.8 %collective-permute-start.37 = (bf16[512,512]{1,0:T(8,128)(2,1)S(1)}, bf16[512,512]{1,0:T(8,128)(2,1)S(1)}, u32[]{:S(2)}, u32[]{:S(2)}) collective-permute-start(bf16[512,512]{1,0:T(8,128)(2,1)S(1)} %add_convert_fusion.5), channel_id=1, source_target_pairs={{0,2},{4,0},{8,4},{12,8},{14,12},{10,14},{6,10},{2,6},{1,3},{5,1},... | collective-permute-start | bytes 1572872 | tf_op jit(solution)/shard_map/ppermute | solution.py:180
  154.4 15.8 %collective-permute-start.19 = (bf16[512,512]{1,0:T(8,128)(2,1)S(1)}, bf16[512,512]{1,0:T(8,128)(2,1)S(1)}, u32[]{:S(2)}, u32[]{:S(2)}) collective-permute-start(bf16[512,512]{1,0:T(8,128)(2,1)S(1)} %convolution_convert_fusion.13), channel_id=1, source_target_pairs={{0,1},{1,0},{2,3},{3,2},{4,5},{5,4},{6,7},{7,6},{8,9},{9,8},{10,11... | collective-permute-start | bytes 1572872 | tf_op jit(solution)/shard_map/ppermute | solution.py:183
  162.8 15.5 %collective-permute-start.23 = (bf16[512,512]{1,0:T(8,128)(2,1)S(1)}, bf16[512,512]{1,0:T(8,128)(2,1)S(1)}, u32[]{:S(2)}, u32[]{:S(2)}) collective-permute-start(bf16[512,512]{1,0:T(8,128)(2,1)S(1)} %add_convert_fusion.12), channel_id=1, source_target_pairs={{0,2},{4,0},{8,4},{12,8},{14,12},{10,14},{6,10},{2,6},{1,3},{5,1},... | collective-permute-start | bytes 1572872 | tf_op jit(solution)/shard_map/ppermute | solution.py:180
  163.3 16.8 %collective-permute-start.26 = (bf16[512,512]{1,0:T(8,128)(2,1)S(1)}, bf16[512,512]{1,0:T(8,128)(2,1)S(1)}, u32[]{:S(2)}, u32[]{:S(2)}) collective-permute-start(bf16[512,512]{1,0:T(8,128)(2,1)S(1)} %convolution_convert_fusion.10), channel_id=1, source_target_pairs={{0,1},{1,0},{2,3},{3,2},{4,5},{5,4},{6,7},{7,6},{8,9},{9,8},{10,11... | collective-permute-start | bytes 1572872 | tf_op jit(solution)/shard_map/ppermute | solution.py:183
  168.4 11.8 %collective-permute-start.30 = (bf16[512,512]{1,0:T(8,128)(2,1)S(1)}, bf16[512,512]{1,0:T(8,128)(2,1)S(1)}, u32[]{:S(2)}, u32[]{:S(2)}) collective-permute-start(bf16[512,512]{1,0:T(8,128)(2,1)S(1)} %add_convert_fusion.8), channel_id=1, source_target_pairs={{0,4},{4,8},{8,12},{12,14},{14,10},{10,6},{6,2},{2,0},{1,5},{5,9},... | collective-permute-start | bytes 1572872 | tf_op jit(solution)/shard_map/ppermute | solution.py:180
  170.2 26.5 %collective-permute-start.32 = (bf16[512,512]{1,0:T(8,128)(2,1)S(1)}, bf16[512,512]{1,0:T(8,128)(2,1)S(1)}, u32[]{:S(2)}, u32[]{:S(2)}) collective-permute-start(bf16[512,512]{1,0:T(8,128)(2,1)S(1)} %convolution_convert_fusion.7), channel_id=1, source_target_pairs={{0,1},{1,0},{2,3},{3,2},{4,5},{5,4},{6,7},{7,6},{8,9},{9,8},{10,11... | collective-permute-start | bytes 1572872 | tf_op jit(solution)/shard_map/ppermute | solution.py:183
  178.3 12.6 %collective-permute-start.45 = (bf16[512,512]{1,0:T(8,128)(2,1)S(1)}, bf16[512,512]{1,0:T(8,128)(2,1)S(1)}, u32[]{:S(2)}, u32[]{:S(2)}) collective-permute-start(bf16[512,512]{1,0:T(8,128)(2,1)S(1)} %add_convert_fusion.1), channel_id=1, source_target_pairs={{0,4},{4,8},{8,12},{12,14},{14,10},{10,6},{6,2},{2,0},{1,5},{5,9},... | collective-permute-start | bytes 1572872 | tf_op jit(solution)/shard_map/ppermute | solution.py:180
  180.1 11.5 %collective-permute-start.18 = (bf16[512,512]{1,0:T(8,128)(2,1)S(1)}, bf16[512,512]{1,0:T(8,128)(2,1)S(1)}, u32[]{:S(2)}, u32[]{:S(2)}) collective-permute-start(bf16[512,512]{1,0:T(8,128)(2,1)S(1)} %convolution_convert_fusion.14), channel_id=1, source_target_pairs={{0,1},{1,0},{2,3},{3,2},{4,5},{5,4},{6,7},{7,6},{8,9},{9,8},{10,11... | collective-permute-start | bytes 1572872 | tf_op jit(solution)/shard_map/ppermute | solution.py:183
  180.2 14.8 %collective-permute-start.24 = (bf16[512,512]{1,0:T(8,128)(2,1)S(1)}, bf16[512,512]{1,0:T(8,128)(2,1)S(1)}, u32[]{:S(2)}, u32[]{:S(2)}) collective-permute-start(bf16[512,512]{1,0:T(8,128)(2,1)S(1)} %add_convert_fusion.11), channel_id=1, source_target_pairs={{0,2},{4,0},{8,4},{12,8},{14,12},{10,14},{6,10},{2,6},{1,3},{5,1},... | collective-permute-start | bytes 1572872 | tf_op jit(solution)/shard_map/ppermute | solution.py:180
  181.0 33.6 %collective-permute-start.17 = (bf16[512,512]{1,0:T(8,128)(2,1)S(1)}, bf16[512,512]{1,0:T(8,128)(2,1)S(1)}, u32[]{:S(2)}, u32[]{:S(2)}) collective-permute-start(bf16[512,512]{1,0:T(8,128)(2,1)S(1)} %convolution_convert_fusion.15), channel_id=1, source_target_pairs={{0,1},{1,0},{2,3},{3,2},{4,5},{5,4},{6,7},{7,6},{8,9},{9,8},{10,11... | collective-permute-start | bytes 1572872 | tf_op jit(solution)/shard_map/ppermute | solution.py:183
  190.9 15.3 %collective-permute-start.38 = (bf16[512,512]{1,0:T(8,128)(2,1)S(1)}, bf16[512,512]{1,0:T(8,128)(2,1)S(1)}, u32[]{:S(2)}, u32[]{:S(2)}) collective-permute-start(bf16[512,512]{1,0:T(8,128)(2,1)S(1)} %add_convert_fusion.4), channel_id=1, source_target_pairs={{0,2},{4,0},{8,4},{12,8},{14,12},{10,14},{6,10},{2,6},{1,3},{5,1},... | collective-permute-start | bytes 1572872 | tf_op jit(solution)/shard_map/ppermute | solution.py:180
  191.6 23.0 %collective-permute-start.31 = (bf16[512,512]{1,0:T(8,128)(2,1)S(1)}, bf16[512,512]{1,0:T(8,128)(2,1)S(1)}, u32[]{:S(2)}, u32[]{:S(2)}) collective-permute-start(bf16[512,512]{1,0:T(8,128)(2,1)S(1)} %add_convert_fusion.7), channel_id=1, source_target_pairs={{0,4},{4,8},{8,12},{12,14},{14,10},{10,6},{6,2},{2,0},{1,5},{5,9},... | collective-permute-start | bytes 1572872 | tf_op jit(solution)/shard_map/ppermute | solution.py:180
  195.0 19.3 %collective-permute-start.46 = (bf16[512,512]{1,0:T(8,128)(2,1)S(1)}, bf16[512,512]{1,0:T(8,128)(2,1)S(1)}, u32[]{:S(2)}, u32[]{:S(2)}) collective-permute-start(bf16[512,512]{1,0:T(8,128)(2,1)S(1)} %add_convert_fusion), channel_id=1, source_target_pairs={{0,4},{4,8},{8,12},{12,14},{14,10},{10,6},{6,2},{2,0},{1,5},{5,9},... | collective-permute-start | bytes 1572872 | tf_op jit(solution)/shard_map/ppermute | solution.py:180
  196.7 20.2 %collective-permute-start.25 = (bf16[512,512]{1,0:T(8,128)(2,1)S(1)}, bf16[512,512]{1,0:T(8,128)(2,1)S(1)}, u32[]{:S(2)}, u32[]{:S(2)}) collective-permute-start(bf16[512,512]{1,0:T(8,128)(2,1)S(1)} %add_convert_fusion.10), channel_id=1, source_target_pairs={{0,2},{4,0},{8,4},{12,8},{14,12},{10,14},{6,10},{2,6},{1,3},{5,1},... | collective-permute-start | bytes 1572872 | tf_op jit(solution)/shard_map/ppermute | solution.py:180
  206.2 21.6 %collective-permute-start.48 = (f32[2,512,512]{2,1,0:T(8,128)}, f32[2,512,512]{2,1,0:T(8,128)}, u32[]{:S(2)}, u32[]{:S(2)}) collective-permute-start(f32[2,512,512]{2,1,0:T(8,128)} %refs_1_.1), channel_id=1, source_target_pairs={{0,1},{1,0},{2,3},{3,2},{4,5},{5,4},{6,7},{7,6},{8,9},{9,8},{10,11... | collective-permute-start | bytes 6291464 | tf_op jit(solution)/shard_map/ppermute | solution.py:183
  214.3 13.6 %collective-permute-start.49 = (f32[2,512,512]{2,1,0:T(8,128)}, f32[2,512,512]{2,1,0:T(8,128)}, u32[]{:S(2)}, u32[]{:S(2)}) collective-permute-start(f32[2,512,512]{2,1,0:T(8,128)} %refs_2_.1), channel_id=1, source_target_pairs={{0,1},{1,0},{2,3},{3,2},{4,5},{5,4},{6,7},{7,6},{8,9},{9,8},{10,11... | collective-permute-start | bytes 6291464 | tf_op jit(solution)/shard_map/ppermute | solution.py:183
  218.5 9.3 %collective-permute-start.47 = (f32[2,512,512]{2,1,0:T(8,128)S(1)}, f32[2,512,512]{2,1,0:T(8,128)}, u32[]{:S(2)}, u32[]{:S(2)}) collective-permute-start(f32[2,512,512]{2,1,0:T(8,128)S(1)} %get-tuple-element.30.refs_0_), channel_id=1, source_target_pairs={{0,1},{1,0},{2,3},{3,2},{4,5},{5,4},{6,7},{7,6},{8,9},{9,8},{10,11... | collective-permute-start | bytes 6291464 | tf_op jit(solution)/shard_map/ppermute | solution.py:183
  (8 other events, 33.9 us)
where the time goes:
time: 243 us; the launch traced here: 242 us
  waiting for transfers between devices  120 us (49%)
  matrix products  41.5 us (17%)
  starting transfers between devices  28.1 us (12%)
  Pallas kernels  18.7 us (8%)
  between operations  13.1 us (5%)
  local copies, waits for them, and re-layouts  10.8 us (4%)
  other arithmetic  9.46 us (4%)
    ppermute x22, waiting for transfers between devices, hop(): lax.ppermute(value, 'blk', [(order[i], order[(i + by) % devices]) for i i...  119 us
    ppermute x22, starting transfers between devices, hop(): lax.ppermute(value, 'blk', [(order[i], order[(i + by) % devices]) for i i...  23.8 us
    dot_general x16, matrix products, rows(): lax.dot_general(other_tokens, other, contract, preferred_element_type=jnp...  15 us
    dot_general x16, matrix products, rows(): lax.dot_general(own_tokens, own, contract, preferred_element_type=jnp.flo...  11.7 us
    pallas_call x1, Pallas kernels, adam_all(): pl.pallas_call(adam_kernel, grid=(pair, units // tile), out_shape=jax.Sha...  10.7 us
    pallas_call x1, Pallas kernels, summed(): pl.pallas_call(functools.partial(total_kernel, devices), out_shape=jax.Sh...  8.04 us
    dot_general x16, matrix products, term(): lax.dot_general(grads[d][which], other_tokens, contract, preferred_elemen...  7.42 us
    dot_general x16, matrix products, term(): lax.dot_general(grads[d][which], own_tokens, contract, preferred_element_...  7.42 us
  transfers between devices with their start and end apart: 50, of which 18 were waited for; matrix products, arithmetic and copies ran while one was open for 19% of the time, Pallas kernels for 3%

commit v1 on v0

--- a/solution.py
+++ b/solution.py
@@ -163,6 +163,167 @@
     )(norm_sq, *own, *other)
 
 
+def gather_kernel(
+    cross, tokens_ref, grad_ref, weights_ref, hidden_ref, out_grads_ref, mine, other, ring_send, ring_recv,
+    cross_send, cross_recv, near_send, near_recv, far_send, far_recv
+):
+    devices = lax.axis_size("blk")
+    half = devices // 2
+    units, features = weights_ref.shape[1], weights_ref.shape[2]
+    token_count = tokens_ref.shape[0]
+    blk, rep, group = lax.axis_index("blk"), lax.axis_index("rep"), lax.axis_index("groups")
+    parity = blk % 2
+    pos = (1 - parity) * (blk // 2) + parity * (devices - 1 - blk // 2)
+
+    def at_position(q):
+        late = q // half
+        return (1 - late) * 2 * q + late * (2 * (devices - 1 - q) + 1)
+
+    after = {"blk": at_position((pos + 1) % devices)}
+    before = {"blk": at_position((pos + devices - 1) % devices)}
+    near = {"rep": 1 - rep}
+    across = {"groups": 1 - group}
+    mesh_ids = pl.DeviceIdType.MESH
+
+    ring_rows = units - cross
+    ring_at = pl.multiple_of((1 - group) * cross, 16)
+    give_at = pl.multiple_of((1 - group) * ring_rows, 16)
+    take_at = pl.multiple_of(group * ring_rows, 16)
+    whole, ring_part = pl.ds(0, units), pl.ds(ring_at, ring_rows)
+    give_part, take_part = pl.ds(give_at, cross), pl.ds(take_at, cross)
+
+    def index_of(direction, k):
+        if k == half:
+            return devices - 1
+        return k if direction > 0 else half - 1 + k
+
+    barrier = pltpu.get_barrier_semaphore()
+    for peer in (after, before, near, across):
+        pl.semaphore_signal(barrier, inc=1, device_id=peer, device_id_type=mesh_ids)
+    pl.semaphore_wait(barrier, 4)
+
+    started = []
+
+    def send(source, target, part, send_sem, recv_sem, peer):
+        copy = pltpu.make_async_remote_copy(
+            src_ref=source.at[part], dst_ref=target.at[part], send_sem=send_sem, recv_sem=recv_sem,
+            device_id=peer, device_id_type=mesh_ids,
+        )
+        copy.start()
+        started.append(copy)
+
+    def arrive(target, part, send_sem, recv_sem, peer):
+        pltpu.make_async_remote_copy(
+            src_ref=target.at[part], dst_ref=target.at[part], send_sem=send_sem, recv_sem=recv_sem,
+            device_id=peer, device_id_type=mesh_ids,
+        ).wait_recv()
+
+    def forward(direction, k, which):
+        if k + 1 == half and which != (0 if direction > 0 else 1):
+            return
+        source = weights_ref.at[which] if k == 0 else mine.at[index_of(direction, k), which]
+        to = index_of(direction, k + 1)
+        send(
+            source, mine.at[to, which], ring_part, ring_send.at[to, which], ring_recv.at[to, which],
+            after if direction > 0 else before,
+        )
+
+    def ring_step(direction, k, which):
+        i = index_of(direction, k)
+        arrive(mine.at[i, which], ring_part, ring_send.at[i, which], ring_recv.at[i, which], after)
+        if k < half:
+            forward(direction, k, which)
+        send(mine.at[i, which], mine.at[i, which], give_part, cross_send.at[i, which], cross_recv.at[i, which], across)
+        send(mine.at[i, which], other.at[i, which], ring_part, near_send.at[i, which], near_recv.at[i, which], near)
+
+    def complete(i):
+        for which in range(2):
+            arrive(mine.at[i, which], take_part, cross_send.at[i, which], cross_recv.at[i, which], across)
+            send(mine.at[i, which], other.at[i, which], take_part, far_send.at[i, which], far_recv.at[i, which], near)
+        for which in range(2):
+            arrive(other.at[i, which], ring_part, near_send.at[i, which], near_recv.at[i, which], near)
+            arrive(other.at[i, which], take_part, far_send.at[i, which], far_recv.at[i, which], near)
+
+    own_at = pl.multiple_of(rep * features, 128)
+    other_at = pl.multiple_of((1 - rep) * features, 128)
+    tile = min(token_count, 256)
+    contract = (((1,), (1,)), ((), ()))
+
+    def compute(i, signed):
+        owner = at_position((pos - signed + devices) % devices)
+        slot = (blk - owner + devices) % devices
+        columns = pl.ds(pl.multiple_of(slot * units, 128), units)
+
+        @pl.loop(0, token_count // tile)
+        def _(t):
+            rows = pl.ds(pl.multiple_of(t * tile, tile), tile)
+            own_tokens = tokens_ref[rows, pl.ds(own_at, features)]
+            other_tokens = tokens_ref[rows, pl.ds(other_at, features)]
+
+            def product(which):
+                own = weights_ref[which] if i == 0 else mine[i, which]
+                return lax.dot_general(own_tokens, own, contract, preferred_element_type=jnp.float32) + lax.dot_general(
+                    other_tokens, other[i, which], contract, preferred_element_type=jnp.float32
+                )
+
+            gate, upper = product(0), product(1)
+            incoming = grad_ref[rows, columns].astype(jnp.float32)
+            sigma = jax.nn.sigmoid(gate)
+            activated = gate * sigma
+            hidden_ref[rows, columns] = (activated * upper).astype(jnp.bfloat16)
+            out_grads_ref[i, 0, rows, :] = (incoming * upper * sigma * (1.0 + gate * (1.0 - sigma))).astype(jnp.bfloat16)
+            out_grads_ref[i, 1, rows, :] = (incoming * activated).astype(jnp.bfloat16)
+
+    for which in range(2):
+        for direction in (1, -1):
+            forward(direction, 0, which)
+    for which in range(2):
+        send(weights_ref.at[which], other.at[0, which], whole, near_send.at[0, which], near_recv.at[0, which], near)
+    for which in range(2):
+        arrive(other.at[0, which], whole, near_send.at[0, which], near_recv.at[0, which], near)
+    compute(0, 0)
+    for k in range(1, half):
+        for which, side in ((0, 1), (1, -1)):
+            for direction in (1, -1):
+                ring_step(direction, k, which)
+            if k > 1:
+                complete(index_of(side, k - 1))
+                compute(index_of(side, k - 1), side * (k - 1))
+    for which, side in ((0, 1), (1, -1)):
+        ring_step(side, half, which)
+        complete(index_of(side, half - 1))
+        compute(index_of(side, half - 1), side * (half - 1))
+    complete(devices - 1)
+    compute(devices - 1, half)
+    for copy in started:
+        copy.wait_send()
+
+
+def gathered_forward(tokens, hidden_grad, weights):
+    devices = lax.axis_size("blk")
+    units, features = weights.shape[1], weights.shape[2]
+    cross = max(16, (units * 5 // 16) // 16 * 16)
+    vmem = pl.BlockSpec(memory_space=pltpu.VMEM)
+    sems = pltpu.SemaphoreType.DMA((devices, 2))
+    return pl.pallas_call(
+        functools.partial(gather_kernel, cross),
+        out_shape=(
+            jax.ShapeDtypeStruct(hidden_grad.shape, jnp.bfloat16),
+            jax.ShapeDtypeStruct((devices, 2, tokens.shape[0], units), jnp.bfloat16),
+        ),
+        in_specs=[vmem] * 3,
+        out_specs=(vmem, vmem),
+        scratch_shapes=[
+            pltpu.VMEM((devices, 2, units, features), jnp.bfloat16),
+            pltpu.VMEM((devices, 2, units, features), jnp.bfloat16),
+        ]
+        + [sems] * 8,
+        compiler_params=pltpu.CompilerParams(
+            collective_id=1, has_side_effects=True, vmem_limit_bytes=56 * 1024 * 1024
+        ),
+    )(tokens, hidden_grad, weights)
+
+
 def ring_order(devices):
     return list(range(0, devices, 2)) + list(range(devices - 1, 0, -2))
 
@@ -170,11 +331,9 @@
 def on_ring(tokens, hidden_grad, weights, first_moment, second_moment):
     devices = lax.axis_size("blk")
     half = devices // 2
-    units, features = weights.shape[1], weights.shape[2]
+    features = weights.shape[2]
     order = ring_order(devices)
-    blk, rep = lax.axis_index("blk"), lax.axis_index("rep")
-    positions = [order.index(i) for i in range(devices)]
-    pos = jnp.array(positions, jnp.int32)[blk]
+    rep = lax.axis_index("rep")
 
     def hop(value, by):
         return lax.ppermute(value, "blk", [(order[i], order[(i + by) % devices]) for i in range(devices)])
@@ -185,42 +344,12 @@
     own_tokens = lax.dynamic_slice_in_dim(tokens, rep * features, features, 1)
     other_tokens = lax.dynamic_slice_in_dim(tokens, (1 - rep) * features, features, 1)
 
-    panels = {0: weights}
-    for k in range(1, half):
-        panels[k] = hop(panels[k - 1], 1)
-        panels[-k] = hop(panels[1 - k], -1)
-    panels[half] = (hop(panels[half - 1][0], 1), hop(panels[1 - half][1], -1))
-
-    def rows(own, other):
-        contract = (((1,), (1,)), ((), ()))
-        return lax.dot_general(own_tokens, own, contract, preferred_element_type=jnp.float32) + lax.dot_general(
-            other_tokens, other, contract, preferred_element_type=jnp.float32
-        )
-
-    def slot_of(distance):
-        owner = jnp.array(order, jnp.int32)[(pos - distance) % devices]
-        return (blk - owner) % devices
-
-    sequence = [0]
-    for k in range(1, half):
-        sequence += [k, -k]
-    sequence.append(half)
-    hidden = jnp.zeros(hidden_grad.shape, hidden_grad.dtype)
-    grads = {}
-    for d in sequence:
-        if d == half:
-            gate_other, up_other = partner(panels[d][0]), partner(panels[d][1])
-        else:
-            gate_other, up_other = partner(panels[d])
-        gate, upper = rows(panels[d][0], gate_other), rows(panels[d][1], up_other)
-        start = slot_of(d) * units
-        incoming = lax.dynamic_slice_in_dim(hidden_grad, start, units, 1).astype(jnp.float32)
-        sigma = jax.nn.sigmoid(gate)
-        activated = gate * sigma
-        hidden = lax.dynamic_update_slice_in_dim(hidden, (activated * upper).astype(jnp.bfloat16), start, 1)
-        gate_grad = (incoming * upper * sigma * (1.0 + gate * (1.0 - sigma))).astype(jnp.bfloat16)
-        up_grad = (incoming * activated).astype(jnp.bfloat16)
-        grads[d] = (gate_grad, up_grad)
+    hidden, slot_grads = gathered_forward(tokens, hidden_grad, weights)
+
+    def index_of(d):
+        return d if d >= 0 and d < half else (devices - 1 if d == half else half - 1 - d)
+
+    grads = {d: slot_grads[index_of(d)] for d in range(1 - half, half + 1)}
 
     def term(d, which):
         contract = (((0,), (0,)), ((), ()))
@@ -264,7 +393,7 @@
 
     def program(tokens, hidden_grad, weights, first_moment, second_moment):
         slots = hidden_grad.shape[1] * devices // weights.shape[1]
-        whole_cycle = slots == devices and devices % 2 == 0 and devices >= 4 and mesh.shape["rep"] == 2
+        whole_cycle = slots == devices and devices % 2 == 0 and devices >= 4 and mesh.shape["rep"] == 2 and mesh.shape["groups"] == 2
         step = jax.shard_map(
             on_ring if whole_cycle else on_device,
             mesh=mesh,

time: 243 us -> 237 us (0.975)
  Pallas kernels: 18.7 us -> 98.4 us
  waiting for transfers between devices: 120 us -> 72 us
  between operations: 13.1 us -> 1.18 us
  starting transfers between devices: 28.1 us -> 19.1 us
  local copies, waits for them, and re-layouts: 10.8 us -> 3.95 us
  matrix products: 41.5 us -> 36.2 us
  other arithmetic: 9.46 us -> 4.85 us
    pallas_call x0 -> x1, Pallas kernels: none -> 79 us  [gathered_forward(): pl.pallas_call(functools.partial(gather_kernel, cross), out_shape=(jax.Sh...]
    ppermute x22 -> x14, waiting for transfers between devices: 119 us -> 71.9 us  [hop(): lax.ppermute(value, 'blk', [(order[i], order[(i + by) % devices]) for i i...]
    dot_general x32 -> x0, matrix products: 26.7 us -> none  [the longest x16 15 us: rows(): lax.dot_general(other_tokens, other, contract, preferred_element_type=jnp...]
    dot_general x16, matrix products: 7.42 us -> 20.1 us  [term(): lax.dot_general(grads[d][which], other_tokens, contract, preferred_elemen...]
    dot_general x16, matrix products: 7.42 us -> 16.1 us  [term(): lax.dot_general(grads[d][which], own_tokens, contract, preferred_element_...]
    ppermute x22 -> x14, starting transfers between devices: 23.8 us -> 16.1 us  [hop(): lax.ppermute(value, 'blk', [(order[i], order[(i + by) % devices]) for i i...]
    convert_element_type x2 -> x0, other arithmetic: 5.06 us -> none  [on_ring(): (incoming * upper * sigma * (1.0 + gate * (1.0 - sigma))).astype(jnp.bflo...]
    dynamic_slice x2 -> x0, local copies, waits for them, and re-layouts: 2.88 us -> none  [the longest x1 1.64 us: slot_of(): owner = jnp.array(order, jnp.int32)[(pos - distance) % devices]]
  transfers between devices with their start and end apart: 50 -> 34, of which waited for: 18 -> 11; matrix products, arithmetic and copies ran while one was open for 19% -> 17% of each run, Pallas kernels for 3% -> 4%
where the time goes in v1:
time: 237 us; the launch traced here: 236 us
  Pallas kernels  98.4 us (42%)
  waiting for transfers between devices  72 us (30%)
  matrix products  36.2 us (15%)
  starting transfers between devices  19.1 us (8%)
  other arithmetic  4.85 us (2%)
  local copies, waits for them, and re-layouts  3.95 us (2%)
    pallas_call x1, Pallas kernels, gathered_forward(): pl.pallas_call(functools.partial(gather_kernel, cross), out_shape=(jax.Sh...  79 us
    ppermute x14, waiting for transfers between devices, hop(): lax.ppermute(value, 'blk', [(order[i], order[(i + by) % devices]) for i i...  71.9 us
    dot_general x16, matrix products, term(): lax.dot_general(grads[d][which], other_tokens, contract, preferred_elemen...  20.1 us
    ppermute x14, starting transfers between devices, hop(): lax.ppermute(value, 'blk', [(order[i], order[(i + by) % devices]) for i i...  16.1 us
    dot_general x16, matrix products, term(): lax.dot_general(grads[d][which], own_tokens, contract, preferred_element_...  16.1 us
    pallas_call x1, Pallas kernels, adam_all(): pl.pallas_call(adam_kernel, grid=(pair, units // tile), out_shape=jax.Sha...  10.9 us
    pallas_call x1, Pallas kernels, summed(): pl.pallas_call(functools.partial(total_kernel, devices), out_shape=jax.Sh...  8.41 us
  transfers between devices with their start and end apart: 34, of which 11 were waited for; matrix products, arithmetic and copies ran while one was open for 17% of the time, Pallas kernels for 4%

profile of v1, /device:TPU:0, one launch (start us, length us, event | category | flops | bytes accessed | tf_op | source)
XLA Modules:
  0.0 235.7 jit_solution(12150711333421543826)
XLA Ops:
  0.6 79.0 %shard_map.68 = (bf16[512,4096]{1,0:T(8,128)(2,1)}, bf16[8,2,512,512]{3,2,1,0:T(8,128)(2,1)}) custom-call(bf16[512,1024]{1,0:T(8,128)(2,1)} %tokens_ref.1, bf16[512,4096]{1,0:T(8,128)(2,1)} %grad_ref.1, bf16[2,512,512]{2,1,0:T(8,128)(2,1)} %refs_3_.1), custom_call_target="tpu_custom_call" | custom-call | tf_op jit(solution)/shard_map/pallas_call | solution.py:308
  79.7 2.5 %convolution_convert_fusion = bf16[512,512]{1,0:T(8,128)(2,1)} fusion(bf16[8,2,512,512]{3,2,1,0:T(8,128)(2,1)} %get-tuple-element.5, bf16[512,1024]{1,0:T(8,128)(2,1)} %tokens_ref.1, s32[]{:T(128)S(6)} %select_n.7), kind=kOutput, calls=%fused_computation.2 | convolution fusion | flops 268697600 | bytes 1572868 | tf_op jit(solution)/shard_map/dot_general | solution.py:356
  82.2 2.5 %convolution_convert_fusion.1 = bf16[512,512]{1,0:T(8,128)(2,1)} fusion(bf16[8,2,512,512]{3,2,1,0:T(8,128)(2,1)} %get-tuple-element.5, bf16[512,1024]{1,0:T(8,128)(2,1)} %tokens_ref.1, s32[]{:T(128)S(6)} %select_n.7), kind=kOutput, calls=%fused_computation.3 | convolution fusion | flops 268697600 | bytes 1572868 | tf_op jit(solution)/shard_map/dot_general | solution.py:356
  85.1 2.3 convolution_convert_fusion.2
  87.5 2.3 convolution_convert_fusion.4
  90.3 2.3 convolution_convert_fusion.5
  92.6 1.5 fusion.6
  94.1 1.7 fusion.9
  95.8 1.5 fusion.12
  97.3 1.5 convolution_convert_fusion.3
  98.8 1.7 fusion.20
  100.5 1.5 fusion.23
  102.0 1.5 convolution_convert_fusion.6
  103.5 1.5 fusion.26
  105.0 1.5 convolution_convert_fusion.7
  112.7 0.6 collective-permute-start.11
  113.2 1.5 add_convert_fusion.3
  114.8 1.5 add_convert_fusion.6
  116.4 0.8 collective-permute-start.26
  117.6 1.4 collective-permute-start.19
  119.5 11.2 %collective-permute-done.26 = bf16[512,512]{1,0:T(8,128)(2,1)S(1)} collective-permute-done((bf16[512,512]{1,0:T(8,128)(2,1)S(1)}, bf16[512,512]{1,0:T(8,128)(2,1)S(1)}, u32[]{:S(2)}, u32[]{:S(2)}) %collective-permute-start.26) | collective-permute-done | bytes 524320 | tf_op jit(solution)/shard_map/ppermute | solution.py:339
  130.7 0.7 collective-permute-start.12
  131.4 1.3 add_convert_fusion.2
  132.8 1.4 collective-permute-start.5
  134.6 9.6 %collective-permute-done.12 = bf16[512,512]{1,0:T(8,128)(2,1)S(1)} collective-permute-done((bf16[512,512]{1,0:T(8,128)(2,1)S(1)}, bf16[512,512]{1,0:T(8,128)(2,1)S(1)}, u32[]{:S(2)}, u32[]{:S(2)}) %collective-permute-start.12) | collective-permute-done | bytes 524320 | tf_op jit(solution)/shard_map/ppermute | solution.py:339
  144.3 0.7 collective-permute-start.27
  145.3 1.8 collective-permute-done.5
  147.1 1.3 collective-permute-start.20
  148.7 8.2 %collective-permute-done.27 = bf16[512,512]{1,0:T(8,128)(2,1)S(1)} collective-permute-done((bf16[512,512]{1,0:T(8,128)(2,1)S(1)}, bf16[512,512]{1,0:T(8,128)(2,1)S(1)}, u32[]{:S(2)}, u32[]{:S(2)}) %collective-permute-start.27) | collective-permute-done | bytes 524320 | tf_op jit(solution)/shard_map/ppermute | solution.py:339
  156.9 1.6 collective-permute-start.6
  158.8 3.1 %collective-permute-done.20 = bf16[512,512]{1,0:T(8,128)(2,1)S(1)} collective-permute-done((bf16[512,512]{1,0:T(8,128)(2,1)S(1)}, bf16[512,512]{1,0:T(8,128)(2,1)S(1)}, u32[]{:S(2)}, u32[]{:S(2)}) %collective-permute-start.20) | collective-permute-done | bytes 524320 | tf_op jit(solution)/shard_map/ppermute | solution.py:339
  162.0 1.4 collective-permute-start.13
  163.7 8.1 %collective-permute-done.6 = bf16[512,512]{1,0:T(8,128)(2,1)S(1)} collective-permute-done((bf16[512,512]{1,0:T(8,128)(2,1)S(1)}, bf16[512,512]{1,0:T(8,128)(2,1)S(1)}, u32[]{:S(2)}, u32[]{:S(2)}) %collective-permute-start.6) | collective-permute-done | bytes 524320 | tf_op jit(solution)/shard_map/ppermute | solution.py:339
  171.8 1.4 collective-permute-start.28
  173.6 1.3 collective-permute-start.7
  175.2 9.2 %collective-permute-done.28 = bf16[512,512]{1,0:T(8,128)(2,1)S(1)} collective-permute-done((bf16[512,512]{1,0:T(8,128)(2,1)S(1)}, bf16[512,512]{1,0:T(8,128)(2,1)S(1)}, u32[]{:S(2)}, u32[]{:S(2)}) %collective-permute-start.28) | collective-permute-done | bytes 524320 | tf_op jit(solution)/shard_map/ppermute | solution.py:339
  184.4 1.5 collective-permute-start.21
  186.7 1.6 collective-permute-done.7
  188.4 1.5 collective-permute-start.29
  191.1 8.5 %collective-permute-done.21 = bf16[512,512]{1,0:T(8,128)(2,1)S(1)} collective-permute-done((bf16[512,512]{1,0:T(8,128)(2,1)S(1)}, bf16[512,512]{1,0:T(8,128)(2,1)S(1)}, u32[]{:S(2)}, u32[]{:S(2)}) %collective-permute-start.21) | collective-permute-done | bytes 524320 | tf_op jit(solution)/shard_map/ppermute | solution.py:339
  199.6 9.5 %collective-permute-done.29 = bf16[512,512]{1,0:T(8,128)(2,1)S(1)} collective-permute-done((bf16[512,512]{1,0:T(8,128)(2,1)S(1)}, bf16[512,512]{1,0:T(8,128)(2,1)S(1)}, u32[]{:S(2)}, u32[]{:S(2)}) %collective-permute-start.29) | collective-permute-done | bytes 524320 | tf_op jit(solution)/shard_map/ppermute | solution.py:339
  209.4 1.0 collective-permute-done.8
  210.6 1.1 pad_maximum_fusion
  212.3 1.2 broadcast_in_dim.3.part_ref
  213.5 8.4 %shard_map.69.norm_ref = f32[8,128]{1,0:T(8,128)} custom-call(f32[8,128]{1,0:T(8,128)} %broadcast_in_dim.3.part_ref), custom_call_target="tpu_custom_call" | custom-call | tf_op jit(solution)/shard_map/pallas_call | solution.py:114
  222.0 0.7 copy-done.1
  222.7 10.9 %shard_map.70 = f32[2,512,1024]{2,1,0:T(8,128)} custom-call(f32[8,128]{1,0:T(8,128)S(1)} %copy-done.1, f32[2,512,512]{2,1,0:T(8,128)S(1)} %get-tuple-element.6.refs_0_, f32[2,512,512]{2,1,0:T(8,128)} %refs_1_.1, f32[2,512,512]{2,1,0:T(8,128)} %refs_2_.1, bf16[2,512,512]{2,1,0:T(8,128)(2,1)S(1)} %copy-done, f32[2,512,512]{2,1,0:T(8,128)} %collective-permute-done.30.refs_4_, ...), custom_call_target="tpu_custom_call" | custom-call | tf_op jit(solution)/shard_map/pallas_call | solution.py:156
  233.6 2.0 copy.8
  (83 shorter events, 13.5 us)
Async XLA Ops:
  0.6 84.5 %copy-start.2 = (bf16[512,1024]{1,0:T(8,128)(2,1)S(1)}, bf16[512,1024]{1,0:T(8,128)(2,1)}, u32[]{:S(2)}) copy-start(bf16[512,1024]{1,0:T(8,128)(2,1)} %tokens_ref.1) | copy-start | bytes 3145732
  82.2 30.5 %collective-permute-start.25 = (bf16[512,512]{1,0:T(8,128)(2,1)}, bf16[512,512]{1,0:T(8,128)(2,1)}, u32[]{:S(2)}, u32[]{:S(2)}) collective-permute-start(bf16[512,512]{1,0:T(8,128)(2,1)} %convolution_convert_fusion), channel_id=1, source_target_pairs={{0,1},{1,0},{2,3},{3,2},{4,5},{5,4},{6,7},{7,6},{8,9},{9,8},{10,11... | collective-permute-start | bytes 1572872 | tf_op jit(solution)/shard_map/ppermute | solution.py:342
  84.6 34.8 %collective-permute-start.24 = (bf16[512,512]{1,0:T(8,128)(2,1)}, bf16[512,512]{1,0:T(8,128)(2,1)}, u32[]{:S(2)}, u32[]{:S(2)}) collective-permute-start(bf16[512,512]{1,0:T(8,128)(2,1)} %convolution_convert_fusion.1), channel_id=1, source_target_pairs={{0,1},{1,0},{2,3},{3,2},{4,5},{5,4},{6,7},{7,6},{8,9},{9,8},{10,11... | collective-permute-start | bytes 1572872 | tf_op jit(solution)/shard_map/ppermute | solution.py:342
  87.5 61.2 %collective-permute-start.23 = (bf16[512,512]{1,0:T(8,128)(2,1)}, bf16[512,512]{1,0:T(8,128)(2,1)S(1)}, u32[]{:S(2)}, u32[]{:S(2)}) collective-permute-start(bf16[512,512]{1,0:T(8,128)(2,1)} %convolution_convert_fusion.2), channel_id=1, source_target_pairs={{0,1},{1,0},{2,3},{3,2},{4,5},{5,4},{6,7},{7,6},{8,9},{9,8},{10,11... | collective-permute-start | bytes 1572872 | tf_op jit(solution)/shard_map/ppermute | solution.py:342
  89.8 25.0 %collective-permute-start.18 = (bf16[512,512]{1,0:T(8,128)(2,1)}, bf16[512,512]{1,0:T(8,128)(2,1)}, u32[]{:S(2)}, u32[]{:S(2)}) collective-permute-start(bf16[512,512]{1,0:T(8,128)(2,1)} %convolution_convert_fusion.4), channel_id=1, source_target_pairs={{0,1},{1,0},{2,3},{3,2},{4,5},{5,4},{6,7},{7,6},{8,9},{9,8},{10,11... | collective-permute-start | bytes 1572872 | tf_op jit(solution)/shard_map/ppermute | solution.py:342
  92.6 40.1 %collective-permute-start.17 = (bf16[512,512]{1,0:T(8,128)(2,1)}, bf16[512,512]{1,0:T(8,128)(2,1)S(1)}, u32[]{:S(2)}, u32[]{:S(2)}) collective-permute-start(bf16[512,512]{1,0:T(8,128)(2,1)} %convolution_convert_fusion.5), channel_id=1, source_target_pairs={{0,1},{1,0},{2,3},{3,2},{4,5},{5,4},{6,7},{7,6},{8,9},{9,8},{10,11... | collective-permute-start | bytes 1572872 | tf_op jit(solution)/shard_map/ppermute | solution.py:342
  94.1 12.4 %slice-start = ((s8[8388608]{0:T(1024)(128)(4,1)}), s8[4194304]{0:T(1024)(128)(4,1)S(1)}, s32[]{:S(2)}) async-start(s8[8388608]{0:T(1024)(128)(4,1)} %bitcast.92), calls=%async_computation | async-start | bytes 8388608
  98.8 7.7 %slice-start.1 = ((s8[8388608]{0:T(1024)(128)(4,1)}), s8[4194304]{0:T(1024)(128)(4,1)S(1)}, s32[]{:S(2)}) async-start(s8[8388608]{0:T(1024)(128)(4,1)} %bitcast.92), calls=%async_computation.1 | async-start | bytes 8388608
  112.7 3.7 %collective-permute-start.11 = (bf16[512,512]{1,0:T(8,128)(2,1)S(1)}, bf16[512,512]{1,0:T(8,128)(2,1)S(1)}, u32[]{:S(2)}, u32[]{:S(2)}) collective-permute-start(bf16[512,512]{1,0:T(8,128)(2,1)S(1)} %convolution_convert_fusion.8), channel_id=1, source_target_pairs={{0,1},{1,0},{2,3},{3,2},{4,5},{5,4},{6,7},{7,6},{8,9},{9,8},{10,11... | collective-permute-start | bytes 1572872 | tf_op jit(solution)/shard_map/ppermute | solution.py:342
  114.8 2.8 %collective-permute-start.4 = (bf16[512,512]{1,0:T(8,128)(2,1)S(1)}, bf16[512,512]{1,0:T(8,128)(2,1)S(1)}, u32[]{:S(2)}, u32[]{:S(2)}) collective-permute-start(bf16[512,512]{1,0:T(8,128)(2,1)S(1)} %convolution_convert_fusion.11), channel_id=1, source_target_pairs={{0,1},{1,0},{2,3},{3,2},{4,5},{5,4},{6,7},{7,6},{8,9},{9,8},{10,11... | collective-permute-start | bytes 1572872 | tf_op jit(solution)/shard_map/ppermute | solution.py:342
  116.4 14.4 %collective-permute-start.26 = (bf16[512,512]{1,0:T(8,128)(2,1)S(1)}, bf16[512,512]{1,0:T(8,128)(2,1)S(1)}, u32[]{:S(2)}, u32[]{:S(2)}) collective-permute-start(bf16[512,512]{1,0:T(8,128)(2,1)S(1)} %add_convert_fusion.3), channel_id=1, source_target_pairs={{0,4},{4,8},{8,12},{12,14},{14,10},{10,6},{6,2},{2,0},{1,5},{5,9},... | collective-permute-start | bytes 1572872 | tf_op jit(solution)/shard_map/ppermute | solution.py:339
  117.6 15.2 %collective-permute-start.19 = (bf16[512,512]{1,0:T(8,128)(2,1)S(1)}, bf16[512,512]{1,0:T(8,128)(2,1)S(1)}, u32[]{:S(2)}, u32[]{:S(2)}) collective-permute-start(bf16[512,512]{1,0:T(8,128)(2,1)S(1)} %add_convert_fusion.6), channel_id=1, source_target_pairs={{0,2},{4,0},{8,4},{12,8},{14,12},{10,14},{6,10},{2,6},{1,3},{5,1},... | collective-permute-start | bytes 1572872 | tf_op jit(solution)/shard_map/ppermute | solution.py:339
  119.5 14.9 %collective-permute-start.10 = (bf16[512,512]{1,0:T(8,128)(2,1)S(1)}, bf16[512,512]{1,0:T(8,128)(2,1)S(1)}, u32[]{:S(2)}, u32[]{:S(2)}) collective-permute-start(bf16[512,512]{1,0:T(8,128)(2,1)S(1)} %convolution_convert_fusion.9), channel_id=1, source_target_pairs={{0,1},{1,0},{2,3},{3,2},{4,5},{5,4},{6,7},{7,6},{8,9},{9,8},{10,11... | collective-permute-start | bytes 1572872 | tf_op jit(solution)/shard_map/ppermute | solution.py:342
  130.7 13.5 %collective-permute-start.12 = (bf16[512,512]{1,0:T(8,128)(2,1)S(1)}, bf16[512,512]{1,0:T(8,128)(2,1)S(1)}, u32[]{:S(2)}, u32[]{:S(2)}) collective-permute-start(bf16[512,512]{1,0:T(8,128)(2,1)S(1)} %add_convert_fusion.9), channel_id=1, source_target_pairs={{0,4},{4,8},{8,12},{12,14},{14,10},{10,6},{6,2},{2,0},{1,5},{5,9},... | collective-permute-start | bytes 1572872 | tf_op jit(solution)/shard_map/ppermute | solution.py:339
  132.7 12.5 %collective-permute-start.3 = (bf16[512,512]{1,0:T(8,128)(2,1)S(1)}, bf16[512,512]{1,0:T(8,128)(2,1)S(1)}, u32[]{:S(2)}, u32[]{:S(2)}) collective-permute-start(bf16[512,512]{1,0:T(8,128)(2,1)S(1)} %convolution_convert_fusion.12), channel_id=1, source_target_pairs={{0,1},{1,0},{2,3},{3,2},{4,5},{5,4},{6,7},{7,6},{8,9},{9,8},{10,11... | collective-permute-start | bytes 1572872 | tf_op jit(solution)/shard_map/ppermute | solution.py:342
  132.8 14.3 %collective-permute-start.5 = (bf16[512,512]{1,0:T(8,128)(2,1)S(1)}, bf16[512,512]{1,0:T(8,128)(2,1)S(1)}, u32[]{:S(2)}, u32[]{:S(2)}) collective-permute-start(bf16[512,512]{1,0:T(8,128)(2,1)S(1)} %add_convert_fusion.13), channel_id=1, source_target_pairs={{0,2},{4,0},{8,4},{12,8},{14,12},{10,14},{6,10},{2,6},{1,3},{5,1},... | collective-permute-start | bytes 1572872 | tf_op jit(solution)/shard_map/ppermute | solution.py:339
  134.4 40.7 %collective-permute-start.22 = (bf16[512,512]{1,0:T(8,128)(2,1)S(1)}, bf16[512,512]{1,0:T(8,128)(2,1)S(1)}, u32[]{:S(2)}, u32[]{:S(2)}) collective-permute-start(bf16[512,512]{1,0:T(8,128)(2,1)S(1)} %convolution_convert_fusion.3), channel_id=1, source_target_pairs={{0,1},{1,0},{2,3},{3,2},{4,5},{5,4},{6,7},{7,6},{8,9},{9,8},{10,11... | collective-permute-start | bytes 1572872 | tf_op jit(solution)/shard_map/ppermute | solution.py:342
  144.3 12.6 %collective-permute-start.27 = (bf16[512,512]{1,0:T(8,128)(2,1)S(1)}, bf16[512,512]{1,0:T(8,128)(2,1)S(1)}, u32[]{:S(2)}, u32[]{:S(2)}) collective-permute-start(bf16[512,512]{1,0:T(8,128)(2,1)S(1)} %add_convert_fusion.2), channel_id=1, source_target_pairs={{0,4},{4,8},{8,12},{12,14},{14,10},{10,6},{6,2},{2,0},{1,5},{5,9},... | collective-permute-start | bytes 1572872 | tf_op jit(solution)/shard_map/ppermute | solution.py:339
  145.2 13.5 %collective-permute-start.16 = (bf16[512,512]{1,0:T(8,128)(2,1)S(1)}, bf16[512,512]{1,0:T(8,128)(2,1)S(1)}, u32[]{:S(2)}, u32[]{:S(2)}) collective-permute-start(bf16[512,512]{1,0:T(8,128)(2,1)S(1)} %convolution_convert_fusion.6), channel_id=1, source_target_pairs={{0,1},{1,0},{2,3},{3,2},{4,5},{5,4},{6,7},{7,6},{8,9},{9,8},{10,11... | collective-permute-start | bytes 1572872 | tf_op jit(solution)/shard_map/ppermute | solution.py:342
  147.1 14.8 %collective-permute-start.20 = (bf16[512,512]{1,0:T(8,128)(2,1)S(1)}, bf16[512,512]{1,0:T(8,128)(2,1)S(1)}, u32[]{:S(2)}, u32[]{:S(2)}) collective-permute-start(bf16[512,512]{1,0:T(8,128)(2,1)S(1)} %add_convert_fusion.5), channel_id=1, source_target_pairs={{0,2},{4,0},{8,4},{12,8},{14,12},{10,14},{6,10},{2,6},{1,3},{5,1},... | collective-permute-start | bytes 1572872 | tf_op jit(solution)/shard_map/ppermute | solution.py:339
  148.7 14.9 %collective-permute-start.2 = (bf16[512,512]{1,0:T(8,128)(2,1)S(1)}, bf16[512,512]{1,0:T(8,128)(2,1)S(1)}, u32[]{:S(2)}, u32[]{:S(2)}) collective-permute-start(bf16[512,512]{1,0:T(8,128)(2,1)S(1)} %convolution_convert_fusion.13), channel_id=1, source_target_pairs={{0,1},{1,0},{2,3},{3,2},{4,5},{5,4},{6,7},{7,6},{8,9},{9,8},{10,11... | collective-permute-start | bytes 1572872 | tf_op jit(solution)/shard_map/ppermute | solution.py:342
  156.9 14.9 %collective-permute-start.6 = (bf16[512,512]{1,0:T(8,128)(2,1)S(1)}, bf16[512,512]{1,0:T(8,128)(2,1)S(1)}, u32[]{:S(2)}, u32[]{:S(2)}) collective-permute-start(bf16[512,512]{1,0:T(8,128)(2,1)S(1)} %add_convert_fusion.12), channel_id=1, source_target_pairs={{0,2},{4,0},{8,4},{12,8},{14,12},{10,14},{6,10},{2,6},{1,3},{5,1},... | collective-permute-start | bytes 1572872 | tf_op jit(solution)/shard_map/ppermute | solution.py:339
  158.7 14.8 %collective-permute-start.9 = (bf16[512,512]{1,0:T(8,128)(2,1)S(1)}, bf16[512,512]{1,0:T(8,128)(2,1)S(1)}, u32[]{:S(2)}, u32[]{:S(2)}) collective-permute-start(bf16[512,512]{1,0:T(8,128)(2,1)S(1)} %convolution_convert_fusion.10), channel_id=1, source_target_pairs={{0,1},{1,0},{2,3},{3,2},{4,5},{5,4},{6,7},{7,6},{8,9},{9,8},{10,11... | collective-permute-start | bytes 1572872 | tf_op jit(solution)/shard_map/ppermute | solution.py:342
  162.0 11.6 %collective-permute-start.13 = (bf16[512,512]{1,0:T(8,128)(2,1)S(1)}, bf16[512,512]{1,0:T(8,128)(2,1)S(1)}, u32[]{:S(2)}, u32[]{:S(2)}) collective-permute-start(bf16[512,512]{1,0:T(8,128)(2,1)S(1)} %add_convert_fusion.8), channel_id=1, source_target_pairs={{0,4},{4,8},{8,12},{12,14},{14,10},{10,6},{6,2},{2,0},{1,5},{5,9},... | collective-permute-start | bytes 1572872 | tf_op jit(solution)/shard_map/ppermute | solution.py:339
  163.6 26.5 %collective-permute-start.15 = (bf16[512,512]{1,0:T(8,128)(2,1)S(1)}, bf16[512,512]{1,0:T(8,128)(2,1)S(1)}, u32[]{:S(2)}, u32[]{:S(2)}) collective-permute-start(bf16[512,512]{1,0:T(8,128)(2,1)S(1)} %convolution_convert_fusion.7), channel_id=1, source_target_pairs={{0,1},{1,0},{2,3},{3,2},{4,5},{5,4},{6,7},{7,6},{8,9},{9,8},{10,11... | collective-permute-start | bytes 1572872 | tf_op jit(solution)/shard_map/ppermute | solution.py:342
  171.8 12.6 %collective-permute-start.28 = (bf16[512,512]{1,0:T(8,128)(2,1)S(1)}, bf16[512,512]{1,0:T(8,128)(2,1)S(1)}, u32[]{:S(2)}, u32[]{:S(2)}) collective-permute-start(bf16[512,512]{1,0:T(8,128)(2,1)S(1)} %add_convert_fusion.1), channel_id=1, source_target_pairs={{0,4},{4,8},{8,12},{12,14},{14,10},{10,6},{6,2},{2,0},{1,5},{5,9},... | collective-permute-start | bytes 1572872 | tf_op jit(solution)/shard_map/ppermute | solution.py:339
  173.5 12.7 %collective-permute-start.1 = (bf16[512,512]{1,0:T(8,128)(2,1)S(1)}, bf16[512,512]{1,0:T(8,128)(2,1)S(1)}, u32[]{:S(2)}, u32[]{:S(2)}) collective-permute-start(bf16[512,512]{1,0:T(8,128)(2,1)S(1)} %convolution_convert_fusion.14), channel_id=1, source_target_pairs={{0,1},{1,0},{2,3},{3,2},{4,5},{5,4},{6,7},{7,6},{8,9},{9,8},{10,11... | collective-permute-start | bytes 1572872 | tf_op jit(solution)/shard_map/ppermute | solution.py:342
  173.6 14.8 %collective-permute-start.7 = (bf16[512,512]{1,0:T(8,128)(2,1)S(1)}, bf16[512,512]{1,0:T(8,128)(2,1)S(1)}, u32[]{:S(2)}, u32[]{:S(2)}) collective-permute-start(bf16[512,512]{1,0:T(8,128)(2,1)S(1)} %add_convert_fusion.11), channel_id=1, source_target_pairs={{0,2},{4,0},{8,4},{12,8},{14,12},{10,14},{6,10},{2,6},{1,3},{5,1},... | collective-permute-start | bytes 1572872 | tf_op jit(solution)/shard_map/ppermute | solution.py:339
  175.1 34.3 %collective-permute-start = (bf16[512,512]{1,0:T(8,128)(2,1)S(1)}, bf16[512,512]{1,0:T(8,128)(2,1)S(1)}, u32[]{:S(2)}, u32[]{:S(2)}) collective-permute-start(bf16[512,512]{1,0:T(8,128)(2,1)S(1)} %convolution_convert_fusion.15), channel_id=1, source_target_pairs={{0,1},{1,0},{2,3},{3,2},{4,5},{5,4},{6,7},{7,6},{8,9},{9,8},{10,11... | collective-permute-start | bytes 1572872 | tf_op jit(solution)/shard_map/ppermute | solution.py:342
  184.4 15.2 %collective-permute-start.21 = (bf16[512,512]{1,0:T(8,128)(2,1)S(1)}, bf16[512,512]{1,0:T(8,128)(2,1)S(1)}, u32[]{:S(2)}, u32[]{:S(2)}) collective-permute-start(bf16[512,512]{1,0:T(8,128)(2,1)S(1)} %add_convert_fusion.4), channel_id=1, source_target_pairs={{0,2},{4,0},{8,4},{12,8},{14,12},{10,14},{6,10},{2,6},{1,3},{5,1},... | collective-permute-start | bytes 1572872 | tf_op jit(solution)/shard_map/ppermute | solution.py:339
  186.2 25.6 %copy-start = (bf16[2,512,512]{2,1,0:T(8,128)(2,1)S(1)}, bf16[2,512,512]{2,1,0:T(8,128)(2,1)}, u32[]{:S(2)}) copy-start(bf16[2,512,512]{2,1,0:T(8,128)(2,1)} %refs_3_.1) | copy-start | bytes 3145732
  186.2 23.2 %collective-permute-start.14 = (bf16[512,512]{1,0:T(8,128)(2,1)S(1)}, bf16[512,512]{1,0:T(8,128)(2,1)S(1)}, u32[]{:S(2)}, u32[]{:S(2)}) collective-permute-start(bf16[512,512]{1,0:T(8,128)(2,1)S(1)} %add_convert_fusion.7), channel_id=1, source_target_pairs={{0,4},{4,8},{8,12},{12,14},{14,10},{10,6},{6,2},{2,0},{1,5},{5,9},... | collective-permute-start | bytes 1572872 | tf_op jit(solution)/shard_map/ppermute | solution.py:339
  188.4 20.7 %collective-permute-start.29 = (bf16[512,512]{1,0:T(8,128)(2,1)S(1)}, bf16[512,512]{1,0:T(8,128)(2,1)S(1)}, u32[]{:S(2)}, u32[]{:S(2)}) collective-permute-start(bf16[512,512]{1,0:T(8,128)(2,1)S(1)} %add_convert_fusion), channel_id=1, source_target_pairs={{0,4},{4,8},{8,12},{12,14},{14,10},{10,6},{6,2},{2,0},{1,5},{5,9},... | collective-permute-start | bytes 1572872 | tf_op jit(solution)/shard_map/ppermute | solution.py:339
  190.1 20.2 %collective-permute-start.8 = (bf16[512,512]{1,0:T(8,128)(2,1)S(1)}, bf16[512,512]{1,0:T(8,128)(2,1)S(1)}, u32[]{:S(2)}, u32[]{:S(2)}) collective-permute-start(bf16[512,512]{1,0:T(8,128)(2,1)S(1)} %add_convert_fusion.10), channel_id=1, source_target_pairs={{0,2},{4,0},{8,4},{12,8},{14,12},{10,14},{6,10},{2,6},{1,3},{5,1},... | collective-permute-start | bytes 1572872 | tf_op jit(solution)/shard_map/ppermute | solution.py:339
  199.6 22.4 %collective-permute-start.31 = (f32[2,512,512]{2,1,0:T(8,128)}, f32[2,512,512]{2,1,0:T(8,128)}, u32[]{:S(2)}, u32[]{:S(2)}) collective-permute-start(f32[2,512,512]{2,1,0:T(8,128)} %refs_1_.1), channel_id=1, source_target_pairs={{0,1},{1,0},{2,3},{3,2},{4,5},{5,4},{6,7},{7,6},{8,9},{9,8},{10,11... | collective-permute-start | bytes 6291464 | tf_op jit(solution)/shard_map/ppermute | solution.py:342
  209.1 12.9 %collective-permute-start.32 = (f32[2,512,512]{2,1,0:T(8,128)}, f32[2,512,512]{2,1,0:T(8,128)}, u32[]{:S(2)}, u32[]{:S(2)}) collective-permute-start(f32[2,512,512]{2,1,0:T(8,128)} %refs_2_.1), channel_id=1, source_target_pairs={{0,1},{1,0},{2,3},{3,2},{4,5},{5,4},{6,7},{7,6},{8,9},{9,8},{10,11... | collective-permute-start | bytes 6291464 | tf_op jit(solution)/shard_map/ppermute | solution.py:342
  211.8 10.2 %collective-permute-start.30 = (f32[2,512,512]{2,1,0:T(8,128)S(1)}, f32[2,512,512]{2,1,0:T(8,128)}, u32[]{:S(2)}, u32[]{:S(2)}) collective-permute-start(f32[2,512,512]{2,1,0:T(8,128)S(1)} %get-tuple-element.6.refs_0_), channel_id=1, source_target_pairs={{0,1},{1,0},{2,3},{3,2},{4,5},{5,4},{6,7},{7,6},{8,9},{9,8},{10,11... | collective-permute-start | bytes 6291464 | tf_op jit(solution)/shard_map/ppermute | solution.py:342
  211.8 10.2 %collective-permute-start.33 = (bf16[2,512,512]{2,1,0:T(8,128)(2,1)S(1)}, bf16[2,512,512]{2,1,0:T(8,128)(2,1)}, u32[]{:S(2)}, u32[]{:S(2)}) collective-permute-start(bf16[2,512,512]{2,1,0:T(8,128)(2,1)S(1)} %copy-done), channel_id=1, source_target_pairs={{0,1},{1,0},{2,3},{3,2},{4,5},{5,4},{6,7},{7,6},{8,9},{9,8},{10,11... | collective-permute-start | bytes 3145736 | tf_op jit(solution)/shard_map/ppermute | solution.py:342
  222.0 0.7 copy-start.1
  222.7 10.9 %copy-start.3 = (bf16[512,4096]{1,0:T(8,128)(2,1)S(1)}, bf16[512,4096]{1,0:T(8,128)(2,1)}, u32[]{:S(2)}) copy-start(bf16[512,4096]{1,0:T(8,128)(2,1)} %get-tuple-element.10) | copy-start | bytes 12582916

commit v2 on v1

--- a/solution.py
+++ b/solution.py
@@ -324,57 +324,149 @@
     )(tokens, hidden_grad, weights)
 
 
-def ring_order(devices):
-    return list(range(0, devices, 2)) + list(range(devices - 1, 0, -2))
-
-
-def on_ring(tokens, hidden_grad, weights, first_moment, second_moment):
+def scatter_kernel(
+    tokens_ref, grads_ref, out_ref, near_out, near_in, ring_out, ring_in, near_send, near_recv, ring_send, ring_recv
+):
     devices = lax.axis_size("blk")
     half = devices // 2
-    features = weights.shape[2]
-    order = ring_order(devices)
-    rep = lax.axis_index("rep")
-
-    def hop(value, by):
-        return lax.ppermute(value, "blk", [(order[i], order[(i + by) % devices]) for i in range(devices)])
-
+    features, units = out_ref.shape[2], out_ref.shape[1]
+    blk, rep = lax.axis_index("blk"), lax.axis_index("rep")
+    parity = blk % 2
+    pos = (1 - parity) * (blk // 2) + parity * (devices - 1 - blk // 2)
+
+    def at_position(q):
+        late = q // half
+        return (1 - late) * 2 * q + late * (2 * (devices - 1 - q) + 1)
+
+    after = {"blk": at_position((pos + 1) % devices)}
+    before = {"blk": at_position((pos + devices - 1) % devices)}
+    near = {"rep": 1 - rep}
+    mesh_ids = pl.DeviceIdType.MESH
+
+    def index_of(direction, k):
+        if k == half:
+            return devices - 1
+        return k if direction > 0 else half - 1 + k
+
+    barrier = pltpu.get_barrier_semaphore()
+    for peer in (after, before, near):
+        pl.semaphore_signal(barrier, inc=1, device_id=peer, device_id_type=mesh_ids)
+    pl.semaphore_wait(barrier, 3)
+
+    started = []
+
+    def near_copy(i, which):
+        return pltpu.make_async_remote_copy(
+            src_ref=near_out.at[i, which], dst_ref=near_in.at[i, which], send_sem=near_send.at[i, which],
+            recv_sem=near_recv.at[i, which], device_id=near, device_id_type=mesh_ids,
+        )
+
+    def ring_copy(i, which, peer):
+        return pltpu.make_async_remote_copy(
+            src_ref=ring_out.at[i, which], dst_ref=ring_in.at[i, which], send_sem=ring_send.at[i, which],
+            recv_sem=ring_recv.at[i, which], device_id=peer, device_id_type=mesh_ids,
+        )
+
+    own_at = pl.multiple_of(rep * features, 128)
+    other_at = pl.multiple_of((1 - rep) * features, 128)
+    tile = min(units, 256)
+    contract = (((0,), (0,)), ((), ()))
+
+    def product(i, which, rows, first):
+        return lax.dot_general(
+            grads_ref[i, which, :, rows], tokens_ref[:, pl.ds(first, features)], contract,
+            preferred_element_type=jnp.float32,
+        )
+
+    def give(i, which):
+        @pl.loop(0, units // tile)
+        def _(t):
+            rows = pl.ds(pl.multiple_of(t * tile, tile), tile)
+            near_out[i, which, rows, :] = product(i, which, rows, other_at).astype(jnp.bfloat16)
+
+        copy = near_copy(i, which)
+        copy.start()
+        started.append(copy)
+
+    def keep(i, which, sources, peer):
+        near_copy(i, which).wait_recv()
+        for source in sources:
+            ring_copy(source, which, after).wait_recv()
+
+        @pl.loop(0, units // tile)
+        def _(t):
+            rows = pl.ds(pl.multiple_of(t * tile, tile), tile)
+            total = product(i, which, rows, own_at) + near_in[i, which, rows, :].astype(jnp.float32)
+            for source in sources:
+                total = total + ring_in[source, which, rows, :].astype(jnp.float32)
+            if peer is None:
+                out_ref[which, rows, :] = total
+            else:
+                ring_out[i, which, rows, :] = total.astype(jnp.bfloat16)
+
+        if peer is not None:
+            copy = ring_copy(i, which, peer)
+            copy.start()
+            started.append(copy)
+
+    def items(k):
+        if k == half:
+            return [(1, 0), (-1, 1)]
+        if k == 0:
+            return [(1, 0), (1, 1)]
+        return [(1, 1), (-1, 0), (1, 0), (-1, 1)]
+
+    for direction, which in items(half):
+        give(index_of(direction, half), which)
+    for k in range(half, -1, -1):
+        if k > 0:
+            following = items(k - 1)
+        for direction, which in items(k):
+            if k == half:
+                sources = []
+            elif k == 0:
+                sources = [index_of(1, 1), index_of(-1, 1)]
+            elif k == half - 1:
+                sources = [devices - 1] if which == (0 if direction > 0 else 1) else []
+            else:
+                sources = [index_of(direction, k + 1)]
+            index = index_of(direction, k) if k > 0 else 0
+            keep(index, which, sources, None if k == 0 else (before if direction > 0 else after))
+            if k == half:
+                continue
+            if k > 0 and following:
+                ahead, part = following.pop(0)
+                give(index_of(ahead, k - 1) if k > 1 else 0, part)
+        if k == half:
+            for ahead, part in items(k - 1):
+                give(index_of(ahead, k - 1), part)
+    for copy in started:
+        copy.wait_send()
+
+
+def reduced_gradient(tokens, slot_grads, features):
+    devices, _, _, units = slot_grads.shape
+    vmem = pl.BlockSpec(memory_space=pltpu.VMEM)
+    sems = pltpu.SemaphoreType.DMA((devices, 2))
+    return pl.pallas_call(
+        scatter_kernel,
+        out_shape=jax.ShapeDtypeStruct((2, units, features), jnp.float32),
+        in_specs=[vmem] * 2,
+        out_specs=vmem,
+        scratch_shapes=[pltpu.VMEM((devices, 2, units, features), jnp.bfloat16)] * 4 + [sems] * 4,
+        compiler_params=pltpu.CompilerParams(
+            collective_id=2, has_side_effects=True, vmem_limit_bytes=56 * 1024 * 1024
+        ),
+    )(tokens, slot_grads)
+
+
+def on_ring(tokens, hidden_grad, weights, first_moment, second_moment):
     def partner(value):
         return lax.ppermute(value, "rep", [(0, 1), (1, 0)])
 
-    own_tokens = lax.dynamic_slice_in_dim(tokens, rep * features, features, 1)
-    other_tokens = lax.dynamic_slice_in_dim(tokens, (1 - rep) * features, features, 1)
-
     hidden, slot_grads = gathered_forward(tokens, hidden_grad, weights)
 
-    def index_of(d):
-        return d if d >= 0 and d < half else (devices - 1 if d == half else half - 1 - d)
-
-    grads = {d: slot_grads[index_of(d)] for d in range(1 - half, half + 1)}
-
-    def term(d, which):
-        contract = (((0,), (0,)), ((), ()))
-        away = lax.dot_general(grads[d][which], other_tokens, contract, preferred_element_type=jnp.float32)
-        kept = lax.dot_general(grads[d][which], own_tokens, contract, preferred_element_type=jnp.float32)
-        return kept + partner(away.astype(jnp.bfloat16)).astype(jnp.float32)
-
-    def chain(sign):
-        running = [None, None]
-        lead = 0 if sign > 0 else 1
-        running[lead] = term(half, lead)
-        arrived = [None, None]
-        arrived[lead] = hop(running[lead].astype(jnp.bfloat16), -sign)
-        for k in range(half - 1, 0, -1):
-            for which in range(2):
-                running[which] = term(sign * k, which)
-                if arrived[which] is not None:
-                    running[which] = running[which] + arrived[which].astype(jnp.float32)
-            arrived = [hop(value.astype(jnp.bfloat16), -sign) for value in running]
-        return arrived
-
-    up_way, down_way = chain(1), chain(-1)
-    gradient = jnp.stack(
-        [term(0, w) + up_way[w].astype(jnp.float32) + down_way[w].astype(jnp.float32) for w in range(2)]
-    )
+    gradient = reduced_gradient(tokens, slot_grads, weights.shape[2])
     norm_sq = summed(jnp.sum(gradient * gradient))
     own = (gradient, first_moment, second_moment, weights)
     update = adam_all(norm_sq, own, tuple(partner(value) for value in own))

time: 237 us -> 200 us (0.84)
  Pallas kernels: 98.4 us -> 191 us
  waiting for transfers between devices: 72 us -> 0.01 us
  matrix products: 36.2 us -> 0 us
  starting transfers between devices: 19.1 us -> 1.09 us
    pallas_call x0 -> x1, Pallas kernels: none -> 92.6 us  [reduced_gradient(): pl.pallas_call(scatter_kernel, out_shape=jax.ShapeDtypeStruct((2, units,...]
    ppermute x14 -> x0, waiting for transfers between devices: 71.9 us -> none  [hop(): lax.ppermute(value, 'blk', [(order[i], order[(i + by) % devices]) for i i...]
    dot_general x32 -> x0, matrix products: 36.2 us -> none  [the longest x16 20.1 us: term(): lax.dot_general(grads[d][which], other_tokens, contract, preferred_elemen...]
    ppermute x14 -> x0, starting transfers between devices: 16.1 us -> none  [hop(): lax.ppermute(value, 'blk', [(order[i], order[(i + by) % devices]) for i i...]
    convert_element_type x10 -> x0, other arithmetic: 3.17 us -> none  [chain(): arrived = [hop(value.astype(jnp.bfloat16), -sign) for value in running]]
    reduce_sum x0 -> x1, other arithmetic: none -> 2.73 us  [on_ring(): norm_sq = summed(jnp.sum(gradient * gradient))]
  transfers between devices with their start and end apart: 34 -> 4, of which waited for: 11 -> 0; matrix products, arithmetic and copies ran while one was open for 17% -> 2% of each run, Pallas kernels for 4% -> 4%
where the time goes in v2:
time: 200 us; the launch traced here: 199 us
  Pallas kernels  191 us (96%)
  local copies, waits for them, and re-layouts  3.94 us (2%)
  other arithmetic  2.73 us (1%)
    pallas_call x1, Pallas kernels, reduced_gradient(): pl.pallas_call(scatter_kernel, out_shape=jax.ShapeDtypeStruct((2, units,...  92.6 us
    pallas_call x1, Pallas kernels, gathered_forward(): pl.pallas_call(functools.partial(gather_kernel, cross), out_shape=(jax.Sh...  78.7 us
    pallas_call x1, Pallas kernels, adam_all(): pl.pallas_call(adam_kernel, grid=(pair, units // tile), out_shape=jax.Sha...  10.9 us
    pallas_call x1, Pallas kernels, summed(): pl.pallas_call(functools.partial(total_kernel, devices), out_shape=jax.Sh...  8.38 us
  transfers between devices with their start and end apart: 4, of which 0 were waited for; matrix products, arithmetic and copies ran while one was open for 2% of the time, Pallas kernels for 4%

profile of v2, /device:TPU:0, one launch (start us, length us, event | category | flops | bytes accessed | tf_op | source)
XLA Modules:
  0.0 199.1 jit_solution(10373040596836120751)
XLA Ops:
  0.6 78.7 %shard_map.68 = (bf16[512,4096]{1,0:T(8,128)(2,1)}, bf16[8,2,512,512]{3,2,1,0:T(8,128)(2,1)}) custom-call(bf16[512,1024]{1,0:T(8,128)(2,1)} %tokens_ref.3, bf16[512,4096]{1,0:T(8,128)(2,1)} %grad_ref.1, bf16[2,512,512]{2,1,0:T(8,128)(2,1)} %refs_3_.1), custom_call_target="tpu_custom_call" | custom-call | tf_op jit(solution)/shard_map/pallas_call | solution.py:308
  79.4 0.0 copy-start.1
  79.4 92.6 %shard_map.69.refs_0_ = f32[2,512,512]{2,1,0:T(8,128)} custom-call(bf16[512,1024]{1,0:T(8,128)(2,1)} %tokens_ref.3, bf16[8,2,512,512]{3,2,1,0:T(8,128)(2,1)} %get-tuple-element.5.grads_ref), custom_call_target="tpu_custom_call" | custom-call | tf_op jit(solution)/shard_map/pallas_call | solution.py:451
  172.0 0.0 copy-start
  172.0 0.2 collective-permute-start
  172.2 0.4 collective-permute-start.1
  172.6 0.1 collective-permute-start.2
  172.7 0.0 copy-done.1
  172.7 0.4 collective-permute-start.3
  173.1 2.7 %multiply_reduce_fusion = f32[]{:T(128)} fusion(f32[2,512,512]{2,1,0:T(8,128)} %shard_map.69.refs_0_), kind=kLoop, calls=%fused_computation | loop fusion | flops 1048575 | bytes 2097156 | tf_op jit(solution)/shard_map/reduce_sum | solution.py:470
  175.8 1.2 broadcast_in_dim.3.part_ref
  177.1 8.4 %shard_map.70.norm_ref = f32[8,128]{1,0:T(8,128)} custom-call(f32[8,128]{1,0:T(8,128)} %broadcast_in_dim.3.part_ref), custom_call_target="tpu_custom_call" | custom-call | tf_op jit(solution)/shard_map/pallas_call | solution.py:114
  185.4 0.0 collective-permute-done.3.refs_7_
  185.5 0.0 collective-permute-done.refs_4_
  185.5 0.0 collective-permute-done.1.refs_5_
  185.5 0.0 collective-permute-done.2.refs_6_
  185.5 0.0 copy-done
  185.5 0.0 copy-start.2
  185.5 0.7 copy-done.2
  186.2 0.0 copy-start.3
  186.2 10.9 %shard_map.71 = f32[2,512,1024]{2,1,0:T(8,128)} custom-call(f32[8,128]{1,0:T(8,128)S(1)} %copy-done.2, f32[2,512,512]{2,1,0:T(8,128)S(1)} %copy-done, f32[2,512,512]{2,1,0:T(8,128)} %refs_1_.1, f32[2,512,512]{2,1,0:T(8,128)} %refs_2_.1, bf16[2,512,512]{2,1,0:T(8,128)(2,1)S(1)} %copy-done.1, f32[2,512,512]{2,1,0:T(8,128)} %collective-permute-done.refs_4_, ...), custom_call_target="tpu_custom_call" | custom-call | tf_op jit(solution)/shard_map/pallas_call | solution.py:156
  197.1 0.0 copy-done.3
  197.1 2.0 %copy.8 = bf16[512,4096]{1,0:T(8,128)(2,1)} copy(bf16[512,4096]{1,0:T(8,128)(2,1)S(1)} %copy-done.3) | data formatting | bytes 8388608
Async XLA Ops:
  79.4 93.3 %copy-start.1 = (bf16[2,512,512]{2,1,0:T(8,128)(2,1)S(1)}, bf16[2,512,512]{2,1,0:T(8,128)(2,1)}, u32[]{:S(2)}) copy-start(bf16[2,512,512]{2,1,0:T(8,128)(2,1)} %refs_3_.1) | copy-start | bytes 3145732
  172.0 13.5 %copy-start = (f32[2,512,512]{2,1,0:T(8,128)S(1)}, f32[2,512,512]{2,1,0:T(8,128)}, u32[]{:S(2)}) copy-start(f32[2,512,512]{2,1,0:T(8,128)} %shard_map.69.refs_0_) | copy-start | bytes 6291460
  172.0 13.5 %collective-permute-start = (f32[2,512,512]{2,1,0:T(8,128)}, f32[2,512,512]{2,1,0:T(8,128)}, u32[]{:S(2)}, u32[]{:S(2)}) collective-permute-start(f32[2,512,512]{2,1,0:T(8,128)} %shard_map.69.refs_0_), channel_id=1, source_target_pairs={{0,1},{1,0},{2,3},{3,2},{4,5},{5,4},{6,7},{7,6},{8,9},{9,8},{10,11... | collective-permute-start | bytes 6291464 | tf_op jit(solution)/shard_map/ppermute | solution.py:465
  172.2 13.3 %collective-permute-start.1 = (f32[2,512,512]{2,1,0:T(8,128)}, f32[2,512,512]{2,1,0:T(8,128)}, u32[]{:S(2)}, u32[]{:S(2)}) collective-permute-start(f32[2,512,512]{2,1,0:T(8,128)} %refs_1_.1), channel_id=1, source_target_pairs={{0,1},{1,0},{2,3},{3,2},{4,5},{5,4},{6,7},{7,6},{8,9},{9,8},{10,11... | collective-permute-start | bytes 6291464 | tf_op jit(solution)/shard_map/ppermute | solution.py:465
  172.6 12.9 %collective-permute-start.2 = (f32[2,512,512]{2,1,0:T(8,128)}, f32[2,512,512]{2,1,0:T(8,128)}, u32[]{:S(2)}, u32[]{:S(2)}) collective-permute-start(f32[2,512,512]{2,1,0:T(8,128)} %refs_2_.1), channel_id=1, source_target_pairs={{0,1},{1,0},{2,3},{3,2},{4,5},{5,4},{6,7},{7,6},{8,9},{9,8},{10,11... | collective-permute-start | bytes 6291464 | tf_op jit(solution)/shard_map/ppermute | solution.py:465
  172.7 12.8 %collective-permute-start.3 = (bf16[2,512,512]{2,1,0:T(8,128)(2,1)S(1)}, bf16[2,512,512]{2,1,0:T(8,128)(2,1)}, u32[]{:S(2)}, u32[]{:S(2)}) collective-permute-start(bf16[2,512,512]{2,1,0:T(8,128)(2,1)S(1)} %copy-done.1), channel_id=1, source_target_pairs={{0,1},{1,0},{2,3},{3,2},{4,5},{5,4},{6,7},{7,6},{8,9},{9,8},{10,11... | collective-permute-start | bytes 3145736 | tf_op jit(solution)/shard_map/ppermute | solution.py:465
  185.5 0.7 copy-start.2
  186.2 10.9 %copy-start.3 = (bf16[512,4096]{1,0:T(8,128)(2,1)S(1)}, bf16[512,4096]{1,0:T(8,128)(2,1)}, u32[]{:S(2)}) copy-start(bf16[512,4096]{1,0:T(8,128)(2,1)} %get-tuple-element.8) | copy-start | bytes 12582916

commit v3 on v2

--- a/solution.py
+++ b/solution.py
@@ -77,64 +77,20 @@
     return (hidden, adam_step)
 
 
-def total_kernel(devices, part_ref, out_ref, slots, send_sem, recv_sem):
-    me = lax.axis_index("blk") * 2 + lax.axis_index("rep")
-
-    def place(by):
-        peer = (me + by) % devices
-        return {"blk": peer // 2, "rep": peer % 2}
-
-    barrier = pltpu.get_barrier_semaphore()
-    for by in range(1, devices):
-        pl.semaphore_signal(barrier, inc=1, device_id=place(by), device_id_type=pl.DeviceIdType.MESH)
-    pl.semaphore_wait(barrier, devices - 1)
-    slots[me] = part_ref[...]
-    copies = []
-    for by in range(1, devices):
-        copy = pltpu.make_async_remote_copy(
-            src_ref=part_ref,
-            dst_ref=slots.at[me],
-            send_sem=send_sem.at[by],
-            recv_sem=recv_sem.at[by],
-            device_id=place(by),
-            device_id_type=pl.DeviceIdType.MESH,
-        )
-        copy.start()
-        copies.append(copy)
-    for copy in copies:
-        copy.wait()
-    total = slots[0]
-    for i in range(1, devices):
-        total = total + slots[i]
-    out_ref[...] = total
-
-
-def summed(value):
-    devices = lax.axis_size("blk") * lax.axis_size("rep")
-    return pl.pallas_call(
-        functools.partial(total_kernel, devices),
-        out_shape=jax.ShapeDtypeStruct((8, 128), jnp.float32),
-        in_specs=[pl.BlockSpec(memory_space=pltpu.VMEM)],
-        out_specs=pl.BlockSpec(memory_space=pltpu.VMEM),
-        scratch_shapes=[
-            pltpu.VMEM((devices, 8, 128), jnp.float32),
-            pltpu.SemaphoreType.DMA((devices,)),
-            pltpu.SemaphoreType.DMA((devices,)),
-        ],
-        compiler_params=pltpu.CompilerParams(collective_id=0, has_side_effects=True),
-    )(jnp.broadcast_to(value, (8, 128)))
-
-
 def adam_kernel(norm_ref, *refs):
     own, other, out_ref = refs[:4], refs[4:8], refs[8]
     features = own[0].shape[-1]
-    norm_sq = norm_ref[0:1, 0:1]
+    scale = jnp.minimum(1.0, clip_norm / jnp.sqrt(norm_ref[0:1, 0:1]))
 
     def write(values, first):
         gradient, first_moment, second_moment, weights = (ref[0] for ref in values)
-        out_ref[0, :, first : first + features] = adam_update(
-            gradient, first_moment, second_moment, weights, norm_sq
-        )
+        clipped = gradient * scale
+        moment = beta_one * first_moment + (1.0 - beta_one) * clipped
+        square = beta_two * second_moment + (1.0 - beta_two) * clipped * clipped
+        moment = moment * (1.0 / (1.0 - beta_one**step_count))
+        square = square * (1.0 / (1.0 - beta_two**step_count))
+        update = moment / (jnp.sqrt(square) + adam_eps) + decay_rate * weights.astype(jnp.float32)
+        out_ref[0, :, first : first + features] = update
 
     rep = lax.axis_index("rep")
 
@@ -325,7 +281,8 @@
 
 
 def scatter_kernel(
-    tokens_ref, grads_ref, out_ref, near_out, near_in, ring_out, ring_in, near_send, near_recv, ring_send, ring_recv
+    tokens_ref, grads_ref, out_ref, other_ref, norm_ref, near_out, near_in, ring_out, ring_in, squares, slots,
+    near_send, near_recv, ring_send, ring_recv, swap_send, swap_recv, norm_send, norm_recv
 ):
     devices = lax.axis_size("blk")
     half = devices // 2
@@ -348,10 +305,18 @@
             return devices - 1
         return k if direction > 0 else half - 1 + k
 
+    members = 2 * devices
+    me = blk * 2 + rep
+
+    def member(by):
+        peer = (me + by) % members
+        return {"blk": peer // 2, "rep": peer % 2}
+
     barrier = pltpu.get_barrier_semaphore()
-    for peer in (after, before, near):
-        pl.semaphore_signal(barrier, inc=1, device_id=peer, device_id_type=mesh_ids)
-    pl.semaphore_wait(barrier, 3)
+    for by in range(1, members):
+        pl.semaphore_signal(barrier, inc=1, device_id=member(by), device_id_type=mesh_ids)
+    pl.semaphore_wait(barrier, members - 1)
+    squares[...] = jnp.zeros_like(squares)
 
     started = []
 
@@ -365,6 +330,12 @@
         return pltpu.make_async_remote_copy(
             src_ref=ring_out.at[i, which], dst_ref=ring_in.at[i, which], send_sem=ring_send.at[i, which],
             recv_sem=ring_recv.at[i, which], device_id=peer, device_id_type=mesh_ids,
+        )
+
+    def swap_copy(which):
+        return pltpu.make_async_remote_copy(
+            src_ref=out_ref.at[which], dst_ref=other_ref.at[which], send_sem=swap_send.at[which],
+            recv_sem=swap_recv.at[which], device_id=near, device_id_type=mesh_ids,
         )
 
     own_at = pl.multiple_of(rep * features, 128)
@@ -401,13 +372,15 @@
                 total = total + ring_in[source, which, rows, :].astype(jnp.float32)
             if peer is None:
                 out_ref[which, rows, :] = total
+                folded = jnp.sum((total * total).reshape(tile // 8, 8, features), axis=0)
+                for lane in range(0, features, 128):
+                    squares[...] += folded[:, lane : lane + 128]
             else:
                 ring_out[i, which, rows, :] = total.astype(jnp.bfloat16)
 
-        if peer is not None:
-            copy = ring_copy(i, which, peer)
-            copy.start()
-            started.append(copy)
+        copy = swap_copy(which) if peer is None else ring_copy(i, which, peer)
+        copy.start()
+        started.append(copy)
 
     def items(k):
         if k == half:
@@ -440,8 +413,25 @@
         if k == half:
             for ahead, part in items(k - 1):
                 give(index_of(ahead, k - 1), part)
+    slots[me] = squares[...]
+    copies = []
+    for by in range(1, members):
+        copy = pltpu.make_async_remote_copy(
+            src_ref=squares, dst_ref=slots.at[me], send_sem=norm_send.at[by], recv_sem=norm_recv.at[by],
+            device_id=member(by), device_id_type=mesh_ids,
+        )
+        copy.start()
+        copies.append(copy)
+    for copy in copies:
+        copy.wait()
+    total = slots[0]
+    for i in range(1, members):
+        total = total + slots[i]
+    norm_ref[...] = jnp.full(norm_ref.shape, jnp.sum(total), jnp.float32)
     for copy in started:
         copy.wait_send()
+    for which in range(2):
+        swap_copy(which).wait_recv()
 
 
 def reduced_gradient(tokens, slot_grads, features):
@@ -450,10 +440,18 @@
     sems = pltpu.SemaphoreType.DMA((devices, 2))
     return pl.pallas_call(
         scatter_kernel,
-        out_shape=jax.ShapeDtypeStruct((2, units, features), jnp.float32),
+        out_shape=(
+            jax.ShapeDtypeStruct((2, units, features), jnp.float32),
+            jax.ShapeDtypeStruct((2, units, features), jnp.float32),
+            jax.ShapeDtypeStruct((8, 128), jnp.float32),
+        ),
         in_specs=[vmem] * 2,
-        out_specs=vmem,
-        scratch_shapes=[pltpu.VMEM((devices, 2, units, features), jnp.bfloat16)] * 4 + [sems] * 4,
+        out_specs=(vmem, pl.BlockSpec(memory_space=pl.ANY), vmem),
+        scratch_shapes=[pltpu.VMEM((devices, 2, units, features), jnp.bfloat16)] * 4
+        + [pltpu.VMEM((8, 128), jnp.float32), pltpu.VMEM((2 * devices, 8, 128), jnp.float32)]
+        + [sems] * 4
+        + [pltpu.SemaphoreType.DMA((2,))] * 2
+        + [pltpu.SemaphoreType.DMA((2 * devices,))] * 2,
         compiler_params=pltpu.CompilerParams(
             collective_id=2, has_side_effects=True, vmem_limit_bytes=56 * 1024 * 1024
         ),
@@ -466,10 +464,10 @@
 
     hidden, slot_grads = gathered_forward(tokens, hidden_grad, weights)
 
-    gradient = reduced_gradient(tokens, slot_grads, weights.shape[2])
-    norm_sq = summed(jnp.sum(gradient * gradient))
-    own = (gradient, first_moment, second_moment, weights)
-    update = adam_all(norm_sq, own, tuple(partner(value) for value in own))
+    gradient, other_gradient, norm_sq = reduced_gradient(tokens, slot_grads, weights.shape[2])
+    own = (first_moment, second_moment, weights)
+    other = tuple(partner(value) for value in own)
+    update = adam_all(norm_sq, (gradient,) + own, (other_gradient,) + other)
     return (hidden, update)
 
 

time: 200 us -> 196 us (0.980)
  Pallas kernels: 191 us -> 188 us
  other arithmetic: 2.73 us -> 0 us
    unnamed x9 -> x15, local copies, waits for them, and re-layouts: 2.7 us -> 5.88 us
    reduce_sum x1 -> x0, other arithmetic: 2.73 us -> none  [on_ring(): norm_sq = summed(jnp.sum(gradient * gradient))]
    pallas_call x2 -> x1, Pallas kernels: 101 us -> 98.6 us  [reduced_gradient(): pl.pallas_call(scatter_kernel, out_shape=(jax.ShapeDtypeStruct((2, units,...]
  transfers between devices with their start and end apart: 4 -> 3, of which waited for: 0 -> 0; matrix products, arithmetic and copies ran while one was open for 2% -> 0% of each run, Pallas kernels for 4% -> 91%
where the time goes in v3:
time: 196 us
  Pallas kernels  188 us (96%)
  local copies, waits for them, and re-layouts  5.88 us (3%)
    pallas_call x1, Pallas kernels, reduced_gradient(): pl.pallas_call(scatter_kernel, out_shape=(jax.ShapeDtypeStruct((2, units,...  98.6 us
    pallas_call x1, Pallas kernels, gathered_forward(): pl.pallas_call(functools.partial(gather_kernel, cross), out_shape=(jax.Sh...  79.8 us
    pallas_call x1, Pallas kernels, adam_all(): pl.pallas_call(adam_kernel, grid=(pair, units // tile), out_shape=jax.Sha...  9.5 us
    unnamed x15, local copies, waits for them, and re-layouts  5.88 us
  transfers between devices with their start and end apart: 3, of which 0 were waited for; matrix products, arithmetic and copies ran while one was open for 0% of the time, Pallas kernels for 91%

profile of v3, /device:TPU:0, one launch (start us, length us, event | category | flops | bytes accessed | tf_op | source)
XLA Modules:
  0.0 195.5 jit_solution(9128478880228117216)
XLA Ops:
  0.6 0.5 collective-permute-start
  1.1 0.1 collective-permute-start.1
  1.2 0.4 collective-permute-start.2
  1.7 79.8 %shard_map.68 = (bf16[512,4096]{1,0:T(8,128)(2,1)}, bf16[8,2,512,512]{3,2,1,0:T(8,128)(2,1)}) custom-call(bf16[512,1024]{1,0:T(8,128)(2,1)} %tokens_ref.3, bf16[512,4096]{1,0:T(8,128)(2,1)} %grad_ref.1, bf16[2,512,512]{2,1,0:T(8,128)(2,1)} %refs_3_.1), custom_call_target="tpu_custom_call" | custom-call | tf_op jit(solution)/shard_map/pallas_call | solution.py:264
  81.4 0.0 copy-start
  81.4 0.0 copy-start.1
  81.5 0.0 copy-start.2
  81.5 98.6 %shard_map.69 = (f32[2,512,512]{2,1,0:T(8,128)}, f32[2,512,512]{2,1,0:T(8,128)}, f32[8,128]{1,0:T(8,128)}) custom-call(bf16[512,1024]{1,0:T(8,128)(2,1)} %tokens_ref.3, bf16[8,2,512,512]{3,2,1,0:T(8,128)(2,1)} %get-tuple-element.8.grads_ref), custom_call_target="tpu_custom_call" | custom-call | tf_op jit(solution)/shard_map/pallas_call | solution.py:441
  180.1 0.0 collective-permute-done.2.refs_7_
  180.1 0.0 collective-permute-done.refs_5_
  180.1 0.0 collective-permute-done.1.refs_6_
  180.1 0.0 copy-done
  180.1 0.0 copy-done.1
  180.1 0.0 copy-done.2
  180.1 0.0 copy-start.3
  180.1 1.6 copy-done.3
  181.7 0.0 copy-start.4
  181.7 1.6 copy-done.4
  183.3 0.0 copy-start.5
  183.3 0.7 copy-done.5
  184.0 0.0 copy-start.6
  184.0 9.5 %shard_map.70 = f32[2,512,1024]{2,1,0:T(8,128)} custom-call(f32[8,128]{1,0:T(8,128)S(1)} %copy-done.5, f32[2,512,512]{2,1,0:T(8,128)S(1)} %copy-done.3, f32[2,512,512]{2,1,0:T(8,128)S(1)} %copy-done.1, f32[2,512,512]{2,1,0:T(8,128)S(1)} %copy-done.2, bf16[2,512,512]{2,1,0:T(8,128)(2,1)S(1)} %copy-done, f32[2,512,512]{2,1,0:T(8,128)S(1)} %copy-done.4, ...), custom_call_target="tpu_custom_call" | custom-call | tf_op jit(solution)/shard_map/pallas_call | solution.py:112
  193.5 0.0 copy-done.6
  193.5 2.0 %copy.8 = bf16[512,4096]{1,0:T(8,128)(2,1)} copy(bf16[512,4096]{1,0:T(8,128)(2,1)S(1)} %copy-done.6) | data formatting | bytes 8388608
Async XLA Ops:
  0.6 179.5 %collective-permute-start = (f32[2,512,512]{2,1,0:T(8,128)}, f32[2,512,512]{2,1,0:T(8,128)S(1)}, u32[]{:S(2)}, u32[]{:S(2)}) collective-permute-start(f32[2,512,512]{2,1,0:T(8,128)} %refs_1_.1), channel_id=1, source_target_pairs={{0,1},{1,0},{2,3},{3,2},{4,5},{5,4},{6,7},{7,6},{8,9},{9,8},{10,11... | collective-permute-start | bytes 6291464 | tf_op jit(solution)/shard_map/ppermute | solution.py:463
  1.1 179.0 %collective-permute-start.1 = (f32[2,512,512]{2,1,0:T(8,128)}, f32[2,512,512]{2,1,0:T(8,128)}, u32[]{:S(2)}, u32[]{:S(2)}) collective-permute-start(f32[2,512,512]{2,1,0:T(8,128)} %refs_2_.1), channel_id=1, source_target_pairs={{0,1},{1,0},{2,3},{3,2},{4,5},{5,4},{6,7},{7,6},{8,9},{9,8},{10,11... | collective-permute-start | bytes 6291464 | tf_op jit(solution)/shard_map/ppermute | solution.py:463
  1.2 178.8 %collective-permute-start.2 = (bf16[2,512,512]{2,1,0:T(8,128)(2,1)}, bf16[2,512,512]{2,1,0:T(8,128)(2,1)}, u32[]{:S(2)}, u32[]{:S(2)}) collective-permute-start(bf16[2,512,512]{2,1,0:T(8,128)(2,1)} %refs_3_.1), channel_id=1, source_target_pairs={{0,1},{1,0},{2,3},{3,2},{4,5},{5,4},{6,7},{7,6},{8,9},{9,8},{10,11... | collective-permute-start | bytes 3145736 | tf_op jit(solution)/shard_map/ppermute | solution.py:463
  81.4 98.7 %copy-start = (bf16[2,512,512]{2,1,0:T(8,128)(2,1)S(1)}, bf16[2,512,512]{2,1,0:T(8,128)(2,1)}, u32[]{:S(2)}) copy-start(bf16[2,512,512]{2,1,0:T(8,128)(2,1)} %refs_3_.1) | copy-start | bytes 3145732
  81.4 98.7 %copy-start.1 = (f32[2,512,512]{2,1,0:T(8,128)S(1)}, f32[2,512,512]{2,1,0:T(8,128)}, u32[]{:S(2)}) copy-start(f32[2,512,512]{2,1,0:T(8,128)} %refs_1_.1) | copy-start | bytes 6291460
  81.5 98.7 %copy-start.2 = (f32[2,512,512]{2,1,0:T(8,128)S(1)}, f32[2,512,512]{2,1,0:T(8,128)}, u32[]{:S(2)}) copy-start(f32[2,512,512]{2,1,0:T(8,128)} %refs_2_.1) | copy-start | bytes 6291460
  180.1 1.6 copy-start.3
  181.7 1.6 copy-start.4
  183.3 0.7 copy-start.5
  184.0 9.5 %copy-start.6 = (bf16[512,4096]{1,0:T(8,128)(2,1)S(1)}, bf16[512,4096]{1,0:T(8,128)(2,1)}, u32[]{:S(2)}) copy-start(bf16[512,4096]{1,0:T(8,128)(2,1)} %get-tuple-element.14) | copy-start | bytes 12582916

commit v4 on v3

--- a/solution.py
+++ b/solution.py
@@ -107,7 +107,7 @@
 
 def adam_all(norm_sq, own, other):
     pair, units, features = own[0].shape
-    tile = min(units, 128)
+    tile = min(units, 256)
     block = pl.BlockSpec((1, tile, features), lambda i, j: (i, j, 0))
     return pl.pallas_call(
         adam_kernel,
@@ -115,7 +115,7 @@
         out_shape=jax.ShapeDtypeStruct((pair, units, 2 * features), jnp.float32),
         in_specs=[pl.BlockSpec((8, 128), lambda i, j: (0, 0))] + [block] * 8,
         out_specs=pl.BlockSpec((1, tile, 2 * features), lambda i, j: (i, j, 0)),
-        compiler_params=pltpu.CompilerParams(vmem_limit_bytes=24 * 1024 * 1024),
+        compiler_params=pltpu.CompilerParams(vmem_limit_bytes=32 * 1024 * 1024),
     )(norm_sq, *own, *other)
 
 
@@ -202,7 +202,7 @@
 
     own_at = pl.multiple_of(rep * features, 128)
     other_at = pl.multiple_of((1 - rep) * features, 128)
-    tile = min(token_count, 256)
+    tile = min(token_count, 512)
     contract = (((1,), (1,)), ((), ()))
 
     def compute(i, signed):

time: 196 us -> 195 us (level)
  transfers between devices with their start and end apart: 3 -> 3, of which waited for: 0 -> 0; matrix products, arithmetic and copies ran while one was open for 0% -> 0% of each run, Pallas kernels for 91% -> 92%
where the time goes in v4:
time: 195 us
  Pallas kernels  187 us (96%)
  local copies, waits for them, and re-layouts  5.88 us (3%)
    pallas_call x1, Pallas kernels, reduced_gradient(): pl.pallas_call(scatter_kernel, out_shape=(jax.ShapeDtypeStruct((2, units,...  98.6 us
    pallas_call x1, Pallas kernels, gathered_forward(): pl.pallas_call(functools.partial(gather_kernel, cross), out_shape=(jax.Sh...  79.6 us
    pallas_call x1, Pallas kernels, adam_all(): pl.pallas_call(adam_kernel, grid=(pair, units // tile), out_shape=jax.Sha...  8.88 us
    unnamed x15, local copies, waits for them, and re-layouts  5.88 us
  transfers between devices with their start and end apart: 3, of which 0 were waited for; matrix products, arithmetic and copies ran while one was open for 0% of the time, Pallas kernels for 92%

profile of v4, /device:TPU:0, one launch (start us, length us, event | category | flops | bytes accessed | tf_op | source)
XLA Modules:
  0.0 194.7 jit_solution(15320033585136740553)
XLA Ops:
  0.6 0.5 collective-permute-start
  1.1 0.1 collective-permute-start.1
  1.2 0.4 collective-permute-start.2
  1.7 79.6 %shard_map.68 = (bf16[512,4096]{1,0:T(8,128)(2,1)}, bf16[8,2,512,512]{3,2,1,0:T(8,128)(2,1)}) custom-call(bf16[512,1024]{1,0:T(8,128)(2,1)} %tokens_ref.3, bf16[512,4096]{1,0:T(8,128)(2,1)} %grad_ref.1, bf16[2,512,512]{2,1,0:T(8,128)(2,1)} %refs_3_.1), custom_call_target="tpu_custom_call" | custom-call | tf_op jit(solution)/shard_map/pallas_call | solution.py:264
  81.3 0.0 copy-start
  81.3 0.0 copy-start.1
  81.3 0.0 copy-start.2
  81.3 98.6 %shard_map.69 = (f32[2,512,512]{2,1,0:T(8,128)}, f32[2,512,512]{2,1,0:T(8,128)}, f32[8,128]{1,0:T(8,128)}) custom-call(bf16[512,1024]{1,0:T(8,128)(2,1)} %tokens_ref.3, bf16[8,2,512,512]{3,2,1,0:T(8,128)(2,1)} %get-tuple-element.8.grads_ref), custom_call_target="tpu_custom_call" | custom-call | tf_op jit(solution)/shard_map/pallas_call | solution.py:441
  179.9 0.0 collective-permute-done.2.refs_7_
  179.9 0.0 collective-permute-done.refs_5_
  179.9 0.0 collective-permute-done.1.refs_6_
  179.9 0.0 copy-done
  179.9 0.0 copy-done.1
  179.9 0.0 copy-done.2
  180.0 0.0 copy-start.3
  180.0 1.6 copy-done.3
  181.5 0.0 copy-start.4
  181.6 1.6 copy-done.4
  183.1 0.0 copy-start.5
  183.1 0.7 copy-done.5
  183.8 0.0 copy-start.6
  183.8 8.9 %shard_map.70 = f32[2,512,1024]{2,1,0:T(8,128)} custom-call(f32[8,128]{1,0:T(8,128)S(1)} %copy-done.5, f32[2,512,512]{2,1,0:T(8,128)S(1)} %copy-done.3, f32[2,512,512]{2,1,0:T(8,128)S(1)} %copy-done.1, f32[2,512,512]{2,1,0:T(8,128)S(1)} %copy-done.2, bf16[2,512,512]{2,1,0:T(8,128)(2,1)S(1)} %copy-done, f32[2,512,512]{2,1,0:T(8,128)S(1)} %copy-done.4, ...), custom_call_target="tpu_custom_call" | custom-call | tf_op jit(solution)/shard_map/pallas_call | solution.py:112
  192.7 0.0 copy-done.6
  192.7 2.0 %copy.8 = bf16[512,4096]{1,0:T(8,128)(2,1)} copy(bf16[512,4096]{1,0:T(8,128)(2,1)S(1)} %copy-done.6) | data formatting | bytes 8388608
Async XLA Ops:
  0.6 179.3 %collective-permute-start = (f32[2,512,512]{2,1,0:T(8,128)}, f32[2,512,512]{2,1,0:T(8,128)S(1)}, u32[]{:S(2)}, u32[]{:S(2)}) collective-permute-start(f32[2,512,512]{2,1,0:T(8,128)} %refs_1_.1), channel_id=1, source_target_pairs={{0,1},{1,0},{2,3},{3,2},{4,5},{5,4},{6,7},{7,6},{8,9},{9,8},{10,11... | collective-permute-start | bytes 6291464 | tf_op jit(solution)/shard_map/ppermute | solution.py:463
  1.1 178.8 %collective-permute-start.1 = (f32[2,512,512]{2,1,0:T(8,128)}, f32[2,512,512]{2,1,0:T(8,128)}, u32[]{:S(2)}, u32[]{:S(2)}) collective-permute-start(f32[2,512,512]{2,1,0:T(8,128)} %refs_2_.1), channel_id=1, source_target_pairs={{0,1},{1,0},{2,3},{3,2},{4,5},{5,4},{6,7},{7,6},{8,9},{9,8},{10,11... | collective-permute-start | bytes 6291464 | tf_op jit(solution)/shard_map/ppermute | solution.py:463
  1.2 178.7 %collective-permute-start.2 = (bf16[2,512,512]{2,1,0:T(8,128)(2,1)}, bf16[2,512,512]{2,1,0:T(8,128)(2,1)}, u32[]{:S(2)}, u32[]{:S(2)}) collective-permute-start(bf16[2,512,512]{2,1,0:T(8,128)(2,1)} %refs_3_.1), channel_id=1, source_target_pairs={{0,1},{1,0},{2,3},{3,2},{4,5},{5,4},{6,7},{7,6},{8,9},{9,8},{10,11... | collective-permute-start | bytes 3145736 | tf_op jit(solution)/shard_map/ppermute | solution.py:463
  81.3 98.7 %copy-start = (bf16[2,512,512]{2,1,0:T(8,128)(2,1)S(1)}, bf16[2,512,512]{2,1,0:T(8,128)(2,1)}, u32[]{:S(2)}) copy-start(bf16[2,512,512]{2,1,0:T(8,128)(2,1)} %refs_3_.1) | copy-start | bytes 3145732
  81.3 98.7 %copy-start.1 = (f32[2,512,512]{2,1,0:T(8,128)S(1)}, f32[2,512,512]{2,1,0:T(8,128)}, u32[]{:S(2)}) copy-start(f32[2,512,512]{2,1,0:T(8,128)} %refs_1_.1) | copy-start | bytes 6291460
  81.3 98.7 %copy-start.2 = (f32[2,512,512]{2,1,0:T(8,128)S(1)}, f32[2,512,512]{2,1,0:T(8,128)}, u32[]{:S(2)}) copy-start(f32[2,512,512]{2,1,0:T(8,128)} %refs_2_.1) | copy-start | bytes 6291460
  180.0 1.6 copy-start.3
  181.5 1.6 copy-start.4
  183.1 0.7 copy-start.5
  183.8 8.9 %copy-start.6 = (bf16[512,4096]{1,0:T(8,128)(2,1)S(1)}, bf16[512,4096]{1,0:T(8,128)(2,1)}, u32[]{:S(2)}) copy-start(bf16[512,4096]{1,0:T(8,128)(2,1)} %get-tuple-element.14) | copy-start | bytes 12582916
